TPU v7x, 768 devices: a whole 4x8x12 slice. The times are simulated.
768 devices in a mesh: lat: 48 (over x, z), lev: 16 (over y, core).
Axes of the slice: x: 4, y: 8, z: 12, core: 2. Of those that a mesh axis runs over, the one named last changes fastest.
Arguments:
- fields: float32 [4, 128, 192, 2048], P(None, 'lev', 'lat'), may hold values from -6 to 6
- courant_lon: float32 [128, 192, 2048], P('lev', 'lat'), may hold values from -0.45 to 0.45
- courant_lat: float32 [128, 192, 2048], P('lev', 'lat'), may hold values from -0.45 to 0.45
- displacement: float32 [128, 192, 2048], P('lev', 'lat'), may hold values from 0 to 0.6
- own_slot: int32 [16, 48, 2], P('lev', 'lat'), may hold values from 0 to 4, as said below
- lent_slot: int32 [16, 48, 2], P('lev', 'lat'), may hold values from 0 to 4, as said below
- w_first: bfloat16 [512, 768], replicated, may hold values from -0.25 to 0.25
- bias_first: float32 [768], replicated, may hold values from -3 to 3
- w_second: bfloat16 [768, 640], replicated, may hold values from -0.21875 to 0.21875
- bias_second: float32 [640], replicated, may hold values from -3 to 3
- w_third: bfloat16 [640, 512], replicated, may hold values from -0.25 to 0.25
- bias_third: float32 [512], replicated, may hold values from -3 to 3
Outputs:
- columns_out: float32 [512, 192, 2048], P(None, 'lat', 'lev')
Inputs may be any that keep to these rules, and one draw needn't show every extreme that they name: own_slot[g, i, s] is a block of band i and group g (0 to 3) handled in work slot s of that band, or 4 when the slot takes no own block; own blocks fill the first slots. lent_slot[g, i, s] is a block of band i and group g handled in work slot s of band (i + 24) mod 48 of group g, or 4; that slot then holds no own block there; no block appears twice in the two lists of its band and group.
All inputs are finite; a program needn't handle non-finite values.
Results may differ from a plain program's by a relative error of at most 0.002.
Values may be sent and summed in bfloat16 or wider, within the bound.
A program may use at most 32 MiB of HBM per device.

v0:
```python
import jax
import jax.numpy as jnp
from jax import lax
from jax.sharding import PartitionSpec as P


def padded_2(value, sides, width):
    for axis, dim in sides:
        count, length = (lax.axis_size(axis), value.shape[dim])
        up = [(i, (i + 1) % count) for i in range(count - 1)]
        down = [(j, i) for i, j in up]
        last = lax.slice_in_dim(value, length - width, length, axis=dim)
        initial = lax.slice_in_dim(value, 0, width, axis=dim)
        before = lax.ppermute(last, axis, up)
        after = lax.ppermute(initial, axis, down)
        value = jnp.concatenate([before, value, after], axis=dim)
    return value


def from_behind(value, axis, by):
    count = lax.axis_size(axis)
    return lax.ppermute(value, axis, [(i, (i + by) % count) for i in range(count)])


def upwind(fields, western, eastern, northern, southern, along_lon, along_lat):
    result = fields - jnp.maximum(along_lon, 0.0) * (fields - western)
    result = result - jnp.minimum(along_lon, 0.0) * (eastern - fields)
    result = result - jnp.maximum(along_lat, 0.0) * (fields - northern)
    return result - jnp.minimum(along_lat, 0.0) * (southern - fields)


def left_product(weight, rows):
    return lax.dot_general(
        weight, rows, (((0,), (0,)), ((), ())), preferred_element_type=jnp.float32
    )


def network(rows, w_first, bias_first, w_second, bias_second, w_third, bias_third):
    hidden = left_product(w_first, rows) + bias_first[:, None]
    hidden = jax.nn.silu(hidden).astype(jnp.bfloat16)
    hidden = left_product(w_second, hidden) + bias_second[:, None]
    hidden = jax.nn.silu(hidden).astype(jnp.bfloat16)
    return (left_product(w_third, hidden) + bias_third[:, None]).astype(jnp.bfloat16)


def body(
    fields,
    courant_lon,
    courant_lat,
    displacement,
    own_slot,
    lent_slot,
    w_first,
    bias_first,
    w_second,
    bias_second,
    w_third,
    bias_third,
):
    field_count, level_part, band_rows, lon_total = fields.shape
    group_count = lax.axis_size("lev")
    band_count = lax.axis_size("lat")
    lon_part = lon_total // group_count
    padded = padded_2(fields, (("lat", 2),), 1)
    advected = upwind(
        fields,
        jnp.roll(fields, 1, axis=3),
        jnp.roll(fields, -1, axis=3),
        padded[:, :, :-2, :],
        padded[:, :, 2:, :],
        courant_lon[None],
        courant_lat[None],
    )
    levels = level_part * group_count

    def split_lon(values):
        return values.reshape(values.shape[0], values.shape[1], band_rows, group_count, lon_part)

    moved, carried = (
        lax.all_to_all(split_lon(advected), "lev", split_axis=3, concat_axis=1, tiled=True),
        lax.all_to_all(
            split_lon(displacement[None]), "lev", split_axis=3, concat_axis=1, tiled=True
        ),
    )
    depth = lax.broadcasted_iota(jnp.int32, (1, levels, 1, 1, 1), 1)
    flux = jnp.where(depth < levels - 1, carried * moved, 0.0)
    above = jnp.concatenate([jnp.zeros_like(flux[:, :1]), flux[:, :-1]], axis=1)
    remapped = moved - flux + above
    width = field_count * levels
    own_list = own_slot.reshape(-1)
    lent_list = lent_slot.reshape(-1)
    work_count = own_list.shape[0]
    block_count = 2 * work_count
    block_rows = band_rows * lon_part // block_count
    blocks = remapped.reshape(width, block_count, block_rows)
    inputs = blocks.astype(jnp.bfloat16)
    block_ids = jnp.arange(block_count, dtype=jnp.int32)[:, None]
    own_hit = own_list[None, :] == block_ids
    lent_hit = lent_list[None, :] == block_ids
    lent_rows = jnp.take(inputs, jnp.minimum(lent_list, block_count - 1), axis=1)
    lent_rows = jnp.where(
        (lent_list < block_count)[None, :, None], lent_rows, jnp.zeros_like(lent_rows)
    )
    arrived = from_behind(lent_rows, "lat", band_count // 2)
    own_rows = jnp.take(inputs, jnp.minimum(own_list, block_count - 1), axis=1)
    work_rows = jnp.where((own_list < block_count)[None, :, None], own_rows, arrived)
    tendency = network(
        work_rows.reshape(width, -1),
        w_first,
        bias_first,
        w_second,
        bias_second,
        w_third,
        bias_third,
    ).reshape(work_rows.shape)
    returned = from_behind(tendency, "lat", band_count // 2)
    added = jnp.einsum(
        "bs,fsc->fbc",
        own_hit.astype(jnp.float32),
        tendency.astype(jnp.float32),
        precision=lax.Precision.HIGHEST,
    )
    added = added + jnp.einsum(
        "bs,fsc->fbc",
        lent_hit.astype(jnp.float32),
        returned.astype(jnp.float32),
        precision=lax.Precision.HIGHEST,
    )
    result = blocks + added
    return result


def solution(mesh):
    in_specs = (
        P(None, "lev", "lat", None),
        P("lev", "lat", None),
        P("lev", "lat", None),
        P("lev", "lat", None),
        P("lev", "lat", None),
        P("lev", "lat", None),
        P(),
        P(),
        P(),
        P(),
        P(),
        P(),
    )
    out_specs = P(None, "lat", "lev")
    return jax.shard_map(body, mesh=mesh, in_specs=in_specs, out_specs=out_specs, check_vma=False)
```

profile of v0, /device:TPU:7, one launch (start us, length us, event | category | flops | bytes accessed | tf_op | source)
XLA Modules:
  0.0 99.8 jit_solution(11672570106066638352)
XLA Ops:
  0.0 2.2 %fusion.32 = (f32[4,8,1,2048]{3,2,1,0:T(1,128)S(1)}, f32[4,8,1,2048]{3,2,1,0:T(1,128)S(1)}) fusion(f32[4,8,4,2048]{3,2,1,0:T(4,128)} %param.14), kind=kLoop, calls=%fused_computation.64 | loop fusion | bytes 1048576 | tf_op jit(solution)/shard_map/slice | solution.py:12
  2.2 0.0 copy-start.3
  2.2 0.1 copy.64
  2.3 4.0 %collective-permute-start = (f32[4,8,1,2048]{3,1,2,0:T(8,128)S(1)}, f32[4,8,1,2048]{3,1,2,0:T(8,128)S(1)}, u32[]{:S(2)}, u32[]{:S(2)}) collective-permute-start(f32[4,8,1,2048]{3,1,2,0:T(8,128)S(1)} %copy.64), channel_id=1, source_target_pairs={{0,16},{16,32},{32,48},{48,64},{64,80},{80,96},{96,112},{112,128},... | collective-permute-start | bytes 786440 | tf_op jit(solution)/shard_map/ppermute | solution.py:14
  6.3 0.0 copy-start.1
  6.3 0.1 copy.65
  6.4 12.6 %collective-permute-start.1 = (f32[4,8,1,2048]{3,1,2,0:T(8,128)S(1)}, f32[4,8,1,2048]{3,1,2,0:T(8,128)}, u32[]{:S(2)}, u32[]{:S(2)}) collective-permute-start(f32[4,8,1,2048]{3,1,2,0:T(8,128)S(1)} %copy.65), channel_id=1, source_target_pairs={{16,0},{32,16},{48,32},{64,48},{80,64},{96,80},{112,96},{128,112},... | collective-permute-start | bytes 786440 | tf_op jit(solution)/shard_map/ppermute | solution.py:15
  19.1 0.1 reshape.119
  19.2 0.9 copy.52
  20.1 8.1 %all-to-all-start.1 = ((f32[1,8,4,16,128]{4,1,2,0,3:T(8,128)}), f32[1,8,4,16,128]{4,1,2,0,3:T(8,128)S(1)}, u32[]{:S(2)}, u32[]{:S(2)}) async-start(f32[1,8,4,16,128]{4,1,2,0,3:T(8,128)} %copy.52), calls=%async_computation.1 | async-start | bytes 524288 | tf_op jit(solution)/shard_map/all_to_all | solution.py:81
  28.1 0.0 copy-start.4
  28.1 0.0 copy-start.5
  28.2 0.7 fusion.30
  28.8 0.3 copy-done.4
  29.1 0.1 copy-done.5
  29.2 0.3 broadcast_maximum_fusion
  29.5 0.1 fusion.31
  29.6 0.3 copy.45
  29.9 1.2 %copy.47 = f32[4,8,1,2048]{3,2,1,0:T(1,128)S(1)} copy(f32[4,8,1,2048]{3,1,2,0:T(8,128)} %collective-permute-done.1) | data formatting | bytes 524288 | tf_op jit(solution)/shard_map/ppermute | solution.py:15
  31.1 2.9 %copy_bitcast_fusion = f32[4,8,4,16,128]{4,2,1,0,3:T(4,128)} fusion(f32[4,8,4,2048]{3,2,1,0:T(4,128)S(1)} %copy-done.1, f32[4,8,1,2048]{3,2,1,0:T(1,128)S(1)} %copy.47, f32[4,8,1,2048]{3,2,1,0:T(1,128)S(1)} %copy.45, f32[4,8,4,2047]{3,2,1,0:T(4,128)S(1)} %get-tuple-element.11, f32[4,8,4,1]{3,2,1,0:T(4,128)S(1)} %get-tuple-element.13, ...), kind=kLoop, calls=%fused_computation.11 | loop fusion | flops 4194304 | bytes 5767168 | tf_op jit(solution)/shard_map/reshape | solution.py:77
  34.0 5.7 %all-to-all-done.1 = f32[1,8,4,16,128]{4,1,2,0,3:T(8,128)S(1)} async-done(((f32[1,8,4,16,128]{4,1,2,0,3:T(8,128)}), f32[1,8,4,16,128]{4,1,2,0,3:T(8,128)S(1)}, u32[]{:S(2)}, u32[]{:S(2)}) %all-to-all-start.1) | async-done | bytes 262176 | tf_op jit(solution)/shard_map/all_to_all | solution.py:81
  39.7 3.6 %all-to-all-start = ((f32[4,8,4,16,128]{4,2,1,0,3:T(4,128)}), f32[4,8,4,16,128]{4,2,1,0,3:T(4,128)S(1)}, u32[]{:S(2)}, u32[]{:S(2)}) async-start(f32[4,8,4,16,128]{4,2,1,0,3:T(4,128)} %copy_bitcast_fusion), calls=%async_computation | async-start | bytes 2097152 | tf_op jit(solution)/shard_map/all_to_all | solution.py:80
  43.3 0.0 copy-start.8
  43.3 0.6 copy-done.8
  44.0 26.6 %all-to-all-done = f32[4,8,4,16,128]{4,2,1,0,3:T(4,128)S(1)} async-done(((f32[4,8,4,16,128]{4,2,1,0,3:T(4,128)}), f32[4,8,4,16,128]{4,2,1,0,3:T(4,128)S(1)}, u32[]{:S(2)}, u32[]{:S(2)}) %all-to-all-start) | async-done | bytes 1048608 | tf_op jit(solution)/shard_map/all_to_all | solution.py:80
  70.5 0.3 fusion.16
  70.8 0.3 fusion.17
  71.1 0.7 copy.54
  71.8 0.2 bitcast_convert_fusion
  72.1 0.1 copy.55
  72.2 0.6 gather_fusion.1
  72.8 0.0 copy-start.7
  72.8 0.1 bitcast_select_fusion
  72.9 2.7 %collective-permute-start.2 = (bf16[512,2,128]{2,0,1:T(8,128)(2,1)S(1)}, bf16[512,2,128]{2,0,1:T(8,128)(2,1)S(1)}, u32[]{:S(2)}, u32[]{:S(2)}) collective-permute-start(bf16[512,2,128]{2,0,1:T(8,128)(2,1)S(1)} %bitcast_select_fusion), channel_id=1, source_target_pairs={{0,384},{16,400},{32,416},{48,432},{64,448},{80,464},{96,480},{112... | collective-permute-start | bytes 786440 | tf_op jit(solution)/shard_map/ppermute | solution.py:22
  75.7 0.6 gather_fusion
  76.3 7.6 %collective-permute-done.2 = bf16[512,2,128]{2,0,1:T(8,128)(2,1)S(1)} collective-permute-done((bf16[512,2,128]{2,0,1:T(8,128)(2,1)S(1)}, bf16[512,2,128]{2,0,1:T(8,128)(2,1)S(1)}, u32[]{:S(2)}, u32[]{:S(2)}) %collective-permute-start.2) | collective-permute-done | bytes 262176 | tf_op jit(solution)/shard_map/ppermute | solution.py:22
  83.9 0.1 bitcast_select_fusion.1
  84.0 0.0 copy-start.9
  84.0 0.1 copy.57
  84.2 0.5 copy-done.9
  84.7 0.0 copy-done.10
  84.7 1.9 %multiply_convert_fusion.1 = bf16[640,256]{0,1:T(8,128)(2,1)S(1)} fusion(bf16[768,640]{1,0:T(8,128)(2,1)S(1)} %copy-done, bf16[512,256]{0,1:T(8,128)(2,1)S(1)} %bitcast.78, bf16[512,768]{1,0:T(8,128)(2,1)} %param.20, f32[768]{0:T(1024)S(1)} %copy-done.9, f32[640]{0:T(1024)S(1)} %copy-done.10), kind=kOutput, calls=%fused_computation.33 | convolution fusion | flops 455147520 | bytes 2364928 | tf_op jit(solution)/shard_map/dot_general | solution.py:33
  86.6 0.4 fusion.4
  87.0 0.2 copy.58
  87.2 2.7 %collective-permute-start.3 = (bf16[512,2,128]{2,1,0:T(2,128)(2,1)S(1)}, bf16[512,2,128]{2,1,0:T(2,128)(2,1)S(1)}, u32[]{:S(2)}, u32[]{:S(2)}) collective-permute-start(bf16[512,2,128]{2,1,0:T(2,128)(2,1)S(1)} %copy.58), channel_id=1, source_target_pairs={{0,384},{16,400},{32,416},{48,432},{64,448},{80,464},{96,480},{112... | collective-permute-start | bytes 786440 | tf_op jit(solution)/shard_map/ppermute | solution.py:22
  89.9 0.6 fusion.21
  90.5 7.7 %collective-permute-done.3 = bf16[512,2,128]{2,1,0:T(2,128)(2,1)S(1)} collective-permute-done((bf16[512,2,128]{2,1,0:T(2,128)(2,1)S(1)}, bf16[512,2,128]{2,1,0:T(2,128)(2,1)S(1)}, u32[]{:S(2)}, u32[]{:S(2)}) %collective-permute-start.3) | collective-permute-done | bytes 262176 | tf_op jit(solution)/shard_map/ppermute | solution.py:22
  98.2 1.6 %fusion.1 = f32[512,4,128]{2,1,0:T(4,128)} fusion(f32[512,4,128]{2,1,0:T(4,128)S(1)} %bitcast.73, f32[512,128,4]{1,2,0:T(4,128)S(1)} %fusion.21, bf16[512,2,128]{2,1,0:T(2,128)(2,1)S(1)} %collective-permute-done.3, s32[2]{0:T(128)S(1)} %bitcast.80), kind=kOutput, calls=%fused_computation.4 | convolution fusion | flops 1572872 | bytes 3407880 | tf_op jit(solution)/shard_map/bs,fsc->fbc/dot_general | solution.py:123
  (18 shorter events, 0.1 us)
Async XLA Ops:
  0.0 84.2 %copy-start = (bf16[768,640]{1,0:T(8,128)(2,1)S(1)}, bf16[768,640]{1,0:T(8,128)(2,1)}, u32[]{:S(2)}) copy-start(bf16[768,640]{1,0:T(8,128)(2,1)} %param.22) | copy-start | bytes 2949124
  2.2 16.8 %copy-start.3 = (f32[8,4,2048]{2,1,0:T(4,128)S(1)}, f32[8,4,2048]{2,1,0:T(4,128)}, u32[]{:S(2)}) copy-start(f32[8,4,2048]{2,1,0:T(4,128)} %param.17) | copy-start | bytes 786436
  2.3 27.3 %collective-permute-start = (f32[4,8,1,2048]{3,1,2,0:T(8,128)S(1)}, f32[4,8,1,2048]{3,1,2,0:T(8,128)S(1)}, u32[]{:S(2)}, u32[]{:S(2)}) collective-permute-start(f32[4,8,1,2048]{3,1,2,0:T(8,128)S(1)} %copy.64), channel_id=1, source_target_pairs={{0,16},{16,32},{32,48},{48,64},{64,80},{80,96},{96,112},{112,128},... | collective-permute-start | bytes 786440 | tf_op jit(solution)/shard_map/ppermute | solution.py:14
  6.3 21.8 %copy-start.1 = (f32[4,8,4,2048]{3,2,1,0:T(4,128)S(1)}, f32[4,8,4,2048]{3,2,1,0:T(4,128)}, u32[]{:S(2)}) copy-start(f32[4,8,4,2048]{3,2,1,0:T(4,128)} %param.14) | copy-start | bytes 3145732
  6.4 23.5 %collective-permute-start.1 = (f32[4,8,1,2048]{3,1,2,0:T(8,128)S(1)}, f32[4,8,1,2048]{3,1,2,0:T(8,128)}, u32[]{:S(2)}, u32[]{:S(2)}) collective-permute-start(f32[4,8,1,2048]{3,1,2,0:T(8,128)S(1)} %copy.65), channel_id=1, source_target_pairs={{16,0},{32,16},{48,32},{64,48},{80,64},{96,80},{112,96},{128,112},... | collective-permute-start | bytes 786440 | tf_op jit(solution)/shard_map/ppermute | solution.py:15
  20.1 19.7 %all-to-all-start.1 = ((f32[1,8,4,16,128]{4,1,2,0,3:T(8,128)}), f32[1,8,4,16,128]{4,1,2,0,3:T(8,128)S(1)}, u32[]{:S(2)}, u32[]{:S(2)}) async-start(f32[1,8,4,16,128]{4,1,2,0,3:T(8,128)} %copy.52), calls=%async_computation.1 | async-start | bytes 524288 | tf_op jit(solution)/shard_map/all_to_all | solution.py:81
  28.1 1.0 copy-start.4
  28.1 1.0 %copy-start.5 = (f32[8,4,2048]{2,1,0:T(4,128)S(1)}, f32[8,4,2048]{2,1,0:T(4,128)}, u32[]{:S(2)}) copy-start(f32[8,4,2048]{2,1,0:T(4,128)} %param.15) | copy-start | bytes 786436
  39.7 30.8 %all-to-all-start = ((f32[4,8,4,16,128]{4,2,1,0,3:T(4,128)}), f32[4,8,4,16,128]{4,2,1,0,3:T(4,128)S(1)}, u32[]{:S(2)}, u32[]{:S(2)}) async-start(f32[4,8,4,16,128]{4,2,1,0,3:T(4,128)} %copy_bitcast_fusion), calls=%async_computation | async-start | bytes 2097152 | tf_op jit(solution)/shard_map/all_to_all | solution.py:80
  43.3 0.7 copy-start.8
  72.8 2.9 %copy-start.7 = (s32[1,1,2]{2,1,0:T(1,128)S(1)}, s32[1,1,2]{2,1,0:T(1,128)}, u32[]{:S(2)}) copy-start(s32[1,1,2]{2,1,0:T(1,128)} %param.18) | copy-start | bytes 28
  72.9 11.0 %collective-permute-start.2 = (bf16[512,2,128]{2,0,1:T(8,128)(2,1)S(1)}, bf16[512,2,128]{2,0,1:T(8,128)(2,1)S(1)}, u32[]{:S(2)}, u32[]{:S(2)}) collective-permute-start(bf16[512,2,128]{2,0,1:T(8,128)(2,1)S(1)} %bitcast_select_fusion), channel_id=1, source_target_pairs={{0,384},{16,400},{32,416},{48,432},{64,448},{80,464},{96,480},{112... | collective-permute-start | bytes 786440 | tf_op jit(solution)/shard_map/ppermute | solution.py:22
  84.0 0.7 copy-start.9
  84.0 0.7 copy-start.10
  84.7 1.9 %copy-start.2 = (bf16[640,512]{1,0:T(8,128)(2,1)S(1)}, bf16[640,512]{1,0:T(8,128)(2,1)}, u32[]{:S(2)}) copy-start(bf16[640,512]{1,0:T(8,128)(2,1)} %param.24) | copy-start | bytes 1966084
  84.7 1.9 %copy-start.6 = (f32[512]{0:T(512)S(1)}, f32[512]{0:T(512)}, u32[]{:S(2)}) copy-start(f32[512]{0:T(512)} %param.25) | copy-start | bytes 6148
  87.2 11.0 %collective-permute-start.3 = (bf16[512,2,128]{2,1,0:T(2,128)(2,1)S(1)}, bf16[512,2,128]{2,1,0:T(2,128)(2,1)S(1)}, u32[]{:S(2)}, u32[]{:S(2)}) collective-permute-start(bf16[512,2,128]{2,1,0:T(2,128)(2,1)S(1)} %copy.58), channel_id=1, source_target_pairs={{0,384},{16,400},{32,416},{48,432},{64,448},{80,464},{96,480},{112... | collective-permute-start | bytes 786440 | tf_op jit(solution)/shard_map/ppermute | solution.py:22
where the time goes:
time: 101 us; the launch traced here: 99.8 us
  waiting for transfers between devices  47.5 us (47%)
  starting transfers between devices  33.7 us (33%)
  local copies, waits for them, and re-layouts  9.42 us (9%)
  matrix products  4.44 us (4%)
  other arithmetic  4.31 us (4%)
    all_to_all x1, waiting for transfers between devices, body(): lax.all_to_all(split_lon(advected), 'lev', split_axis=3, concat_axis=1, t...  26.6 us
    ppermute x2, waiting for transfers between devices, from_behind(): lax.ppermute(value, axis, [(i, (i + by) % count) for i in range(count)])  15.3 us
    ppermute x1, starting transfers between devices, padded_2(): after = lax.ppermute(initial, axis, down)  12.6 us
    all_to_all x1, starting transfers between devices, body(): lax.all_to_all(split_lon(displacement[None]), 'lev', split_axis=3, concat...  8.07 us
    all_to_all x1, waiting for transfers between devices, body(): lax.all_to_all(split_lon(displacement[None]), 'lev', split_axis=3, concat...  5.69 us
    ppermute x2, starting transfers between devices, from_behind(): lax.ppermute(value, axis, [(i, (i + by) % count) for i in range(count)])  5.48 us
    ppermute x1, starting transfers between devices, padded_2(): before = lax.ppermute(last, axis, up)  4 us
    all_to_all x1, starting transfers between devices, body(): lax.all_to_all(split_lon(advected), 'lev', split_axis=3, concat_axis=1, t...  3.55 us
  transfers between devices with their start and end apart: 6, of which 4 were waited for; matrix products, arithmetic and copies ran while one was open for 8% of the time, Pallas kernels for 0%

commit v1 on v0

v1 whole, which is shorter than its diff:
```python
import jax
import jax.numpy as jnp
from jax import lax
from jax.sharding import PartitionSpec as P


def padded_lat(value):
    count, length = lax.axis_size("lat"), value.shape[2]
    up = [(i, i + 1) for i in range(count - 1)]
    down = [(j, i) for i, j in up]
    ends = value.astype(jnp.bfloat16)
    last = lax.slice_in_dim(ends, length - 1, length, axis=2)
    first = lax.slice_in_dim(ends, 0, 1, axis=2)
    before = lax.ppermute(last, "lat", up).astype(value.dtype)
    after = lax.ppermute(first, "lat", down).astype(value.dtype)
    return jnp.concatenate([before, value, after], axis=2)


def upwind(fields, western, eastern, northern, southern, along_lon, along_lat):
    result = fields - jnp.maximum(along_lon, 0.0) * (fields - western)
    result = result - jnp.minimum(along_lon, 0.0) * (eastern - fields)
    result = result - jnp.maximum(along_lat, 0.0) * (fields - northern)
    return result - jnp.minimum(along_lat, 0.0) * (southern - fields)


def left_product(weight, rows):
    return lax.dot_general(
        weight, rows, (((0,), (0,)), ((), ())), preferred_element_type=jnp.float32
    )


def network(rows, w_first, bias_first, w_second, bias_second, w_third, bias_third):
    hidden = left_product(w_first, rows) + bias_first[:, None]
    hidden = jax.nn.silu(hidden).astype(jnp.bfloat16)
    hidden = left_product(w_second, hidden) + bias_second[:, None]
    hidden = jax.nn.silu(hidden).astype(jnp.bfloat16)
    return left_product(w_third, hidden) + bias_third[:, None]


def body(
    fields,
    courant_lon,
    courant_lat,
    displacement,
    own_slot,
    lent_slot,
    w_first,
    bias_first,
    w_second,
    bias_second,
    w_third,
    bias_third,
):
    field_count, level_part, band_rows, lon_total = fields.shape
    group_count = lax.axis_size("lev")
    lon_part = lon_total // group_count
    padded = padded_lat(fields)
    advected = upwind(
        fields,
        jnp.roll(fields, 1, axis=3),
        jnp.roll(fields, -1, axis=3),
        padded[:, :, :-2, :],
        padded[:, :, 2:, :],
        courant_lon[None],
        courant_lat[None],
    )
    flux = displacement[None] * advected
    lowest = flux[:, level_part - 1 :].astype(jnp.bfloat16)
    steps = [(i, i + 1) for i in range(group_count - 1)]
    entering = lax.ppermute(lowest, "lev", steps).astype(jnp.float32)
    depth = lax.broadcasted_iota(jnp.int32, (1, level_part, 1, 1), 1)
    bottom = lax.axis_index("lev") * level_part + depth == group_count * level_part - 1
    above = jnp.concatenate([entering, flux[:, : level_part - 1]], axis=1)
    remapped = advected - jnp.where(bottom, 0.0, flux) + above
    split = remapped.astype(jnp.bfloat16).reshape(
        field_count, level_part, band_rows, group_count, lon_part
    )
    moved = lax.all_to_all(split, "lev", split_axis=3, concat_axis=1, tiled=True)
    width = field_count * level_part * group_count
    rows = moved.reshape(width, band_rows * lon_part)
    tendency = network(
        rows, w_first, bias_first, w_second, bias_second, w_third, bias_third
    )
    slots = jnp.concatenate([own_slot.reshape(-1), lent_slot.reshape(-1)])
    block_ids = jnp.arange(band_rows, dtype=jnp.int32)
    active = jnp.any(slots[None, :] == block_ids[:, None], axis=1)
    shape = (width, band_rows, lon_part)
    added = jnp.where(active[None, :, None], tendency.reshape(shape), 0.0)
    return rows.reshape(shape).astype(jnp.float32) + added


def solution(mesh):
    in_specs = (
        P(None, "lev", "lat", None),
        P("lev", "lat", None),
        P("lev", "lat", None),
        P("lev", "lat", None),
        P("lev", "lat", None),
        P("lev", "lat", None),
        P(),
        P(),
        P(),
        P(),
        P(),
        P(),
    )
    out_specs = P(None, "lat", "lev")
    return jax.shard_map(body, mesh=mesh, in_specs=in_specs, out_specs=out_specs, check_vma=False)
```

time: 101 us -> 73.3 us (0.73)
  waiting for transfers between devices: 47.5 us -> 18.6 us
  other arithmetic: 4.31 us -> 11.1 us
  starting transfers between devices: 33.7 us -> 30.7 us
  local copies, waits for them, and re-layouts: 9.42 us -> 7.33 us
    all_to_all x2 -> x1, waiting for transfers between devices: 32.2 us -> 17 us  [body(): lax.all_to_all(split, 'lev', split_axis=3, concat_axis=1, tiled=True)]
    ppermute x4 -> x3, waiting for transfers between devices: 15.3 us -> 1.58 us  [the longest x1 1.22 us: body(): entering = lax.ppermute(lowest, 'lev', steps).astype(jnp.float32)]
    convert_element_type x1 -> x4, other arithmetic: 0.25 us -> 4.04 us  [the longest x1 1.59 us: padded_lat(): ends = value.astype(jnp.bfloat16)]
    mul x0 -> x1, other arithmetic: none -> 3.29 us  [body(): flux = displacement[None] * advected]
    dot_general x2, matrix products: 2.26 us -> 4.94 us  [left_product(): lax.dot_general(weight, rows, (((0,), (0,)), ((), ())), preferred_element...]
    dot_general x2 -> x0, matrix products: 2.18 us -> none  [the longest x1 1.63 us: body(): jnp.einsum('bs,fsc->fbc', lent_hit.astype(jnp.float32), returned.astype(j...]
    all_to_all x2 -> x1, starting transfers between devices: 11.6 us -> 9.63 us  [body(): lax.all_to_all(split, 'lev', split_axis=3, concat_axis=1, tiled=True)]
    max x1, other arithmetic: 0.3 us -> 2.13 us  [upwind(): result = result - jnp.maximum(along_lat, 0.0) * (fields - northern)]
  transfers between devices with their start and end apart: 6 -> 4, of which waited for: 4 -> 3; matrix products, arithmetic and copies ran while one was open for 8% -> 7% of each run, Pallas kernels for 0% -> 0%
where the time goes in v1:
time: 73.3 us; the launch traced here: 72.8 us
  starting transfers between devices  30.7 us (42%)
  waiting for transfers between devices  18.6 us (25%)
  other arithmetic  11.1 us (15%)
  local copies, waits for them, and re-layouts  7.33 us (10%)
  matrix products  4.94 us (7%)
    all_to_all x1, waiting for transfers between devices, body(): lax.all_to_all(split, 'lev', split_axis=3, concat_axis=1, tiled=True)  17 us
    ppermute x1, starting transfers between devices, padded_lat(): after = lax.ppermute(first, 'lat', down).astype(value.dtype)  12.6 us
    all_to_all x1, starting transfers between devices, body(): lax.all_to_all(split, 'lev', split_axis=3, concat_axis=1, tiled=True)  9.63 us
    dot_general x2, matrix products, left_product(): lax.dot_general(weight, rows, (((0,), (0,)), ((), ())), preferred_element...  4.94 us
    ppermute x1, starting transfers between devices, body(): entering = lax.ppermute(lowest, 'lev', steps).astype(jnp.float32)  4.43 us
    ppermute x1, starting transfers between devices, padded_lat(): before = lax.ppermute(last, 'lat', up).astype(value.dtype)  3.99 us
    mul x1, other arithmetic, body(): flux = displacement[None] * advected  3.29 us
    max x1, other arithmetic, upwind(): result = result - jnp.maximum(along_lat, 0.0) * (fields - northern)  2.13 us
  transfers between devices with their start and end apart: 4, of which 3 were waited for; matrix products, arithmetic and copies ran while one was open for 7% of the time, Pallas kernels for 0%

profile of v1, /device:TPU:7, one launch (start us, length us, event | category | flops | bytes accessed | tf_op | source)
XLA Modules:
  0.0 72.8 jit_solution(8671686403981092887)
XLA Ops:
  0.0 0.0 copy-start
  0.0 0.0 copy-start.1
  0.0 1.6 %convert_element_type.28 = bf16[4,8,4,2048]{3,2,1,0:T(4,128)(2,1)S(1)} convert(f32[4,8,4,2048]{3,2,1,0:T(4,128)} %param.12) | non-fusion elementwise | flops 262144 | bytes 1572864 | tf_op jit(solution)/shard_map/convert_element_type | solution.py:11
  1.6 1.2 %fusion.25 = (bf16[4,8,1,2048]{3,2,1,0:T(2,128)(2,1)}, bf16[4,8,1,2048]{3,2,1,0:T(2,128)(2,1)}) fusion(bf16[4,8,4,2048]{3,2,1,0:T(4,128)(2,1)S(1)} %convert_element_type.28), kind=kLoop, calls=%fused_computation.46 | loop fusion | bytes 524288 | tf_op jit(solution)/shard_map/slice | solution.py:12
  2.8 4.0 %collective-permute-start = (bf16[4,8,1,2048]{3,2,1,0:T(2,128)(2,1)}, bf16[4,8,1,2048]{3,2,1,0:T(2,128)(2,1)}, u32[]{:S(2)}, u32[]{:S(2)}) collective-permute-start(bf16[4,8,1,2048]{3,2,1,0:T(2,128)(2,1)} %get-tuple-element.13), channel_id=1, source_target_pairs={{0,16},{16,32},{32,48},{48,64},{64,80},{80,96},{96,112},{112,128},... | collective-permute-start | bytes 393224 | tf_op jit(solution)/shard_map/ppermute | solution.py:14
  6.8 0.0 copy-start.4
  6.8 12.6 %collective-permute-start.1 = (bf16[4,8,1,2048]{3,2,1,0:T(2,128)(2,1)}, bf16[4,8,1,2048]{3,2,1,0:T(2,128)(2,1)}, u32[]{:S(2)}, u32[]{:S(2)}) collective-permute-start(bf16[4,8,1,2048]{3,2,1,0:T(2,128)(2,1)} %get-tuple-element.14), channel_id=1, source_target_pairs={{16,0},{32,16},{48,32},{64,48},{80,64},{96,80},{112,96},{128,112},... | collective-permute-start | bytes 393224 | tf_op jit(solution)/shard_map/ppermute | solution.py:15
  19.4 0.0 copy-done.1
  19.4 1.6 %fusion.23 = (f32[4,8,4,2047]{3,2,1,0:T(4,128)S(1)}, f32[4,8,4,2047]{3,2,1,0:T(4,128)}) fusion(f32[4,8,4,2048]{3,2,1,0:T(4,128)S(1)} %copy-done.1), kind=kLoop, calls=%fused_computation.44 | loop fusion | bytes 4192256 | tf_op jit(solution)/shard_map/jit(_roll_static)/slice | solution.py:60
  21.1 0.0 copy-done.4
  21.1 2.1 %broadcast_maximum_fusion = (f32[8,4,2048]{2,1,0:T(4,128)}, f32[8,4,2048]{2,1,0:T(4,128)}, f32[8,4,2048]{2,1,0:T(4,128)}, f32[8,4,2048]{2,1,0:T(4,128)}) fusion(f32[8,4,2048]{2,1,0:T(4,128)S(1)} %copy-done.4, f32[8,4,2048]{2,1,0:T(4,128)} %param.13), kind=kLoop, calls=%fused_computation.34 | loop fusion | flops 262144 | bytes 1572864 | tf_op jit(solution)/shard_map/max | solution.py:22
  23.2 0.0 copy-start.3
  23.2 0.0 copy-start.2
  23.2 0.1 fusion.22
  23.3 0.4 collective-permute-done
  23.7 1.2 %convert_element_type.29 = f32[4,8,1,2048]{3,2,1,0:T(1,128)S(1)} convert(bf16[4,8,1,2048]{3,2,1,0:T(2,128)(2,1)} %collective-permute-done) | non-fusion elementwise | flops 65536 | bytes 393216 | tf_op jit(solution)/shard_map/convert_element_type | solution.py:14
  24.9 0.0 collective-permute-done.1
  24.9 1.2 %convert_element_type.30 = f32[4,8,1,2048]{3,2,1,0:T(1,128)S(1)} convert(bf16[4,8,1,2048]{3,2,1,0:T(2,128)(2,1)} %collective-permute-done.1) | non-fusion elementwise | flops 65536 | bytes 393216 | tf_op jit(solution)/shard_map/convert_element_type | solution.py:15
  26.1 0.0 copy-done.3
  26.1 0.0 copy-done.2
  26.1 3.3 %broadcast_multiply_fusion = (f32[4,8,4,2048]{3,2,1,0:T(4,128)S(1)}, f32[4,8,4,2048]{3,2,1,0:T(4,128)S(1)}) fusion(f32[8,4,2048]{2,1,0:T(4,128)S(1)} %copy-done.3, f32[4,8,4,2048]{3,2,1,0:T(4,128)S(1)} %copy-done.1, f32[4,8,1,2048]{3,2,1,0:T(1,128)S(1)} %convert_element_type.30, f32[8,4,2048]{2,1,0:T(4,128)} %get-tuple-element.18, ...), kind=kLoop, calls=%fused_computation.30 | loop fusion | flops 4456448 | bytes 7077888 | tf_op jit(solution)/shard_map/mul | solution.py:67
  29.5 4.4 %collective-permute-start.2 = (bf16[4,1,4,2048]{3,2,1,0:T(4,128)(2,1)S(1)}, bf16[4,1,4,2048]{3,2,1,0:T(4,128)(2,1)S(1)}, u32[]{:S(2)}, u32[]{:S(2)}) collective-permute-start(bf16[4,1,4,2048]{3,2,1,0:T(4,128)(2,1)S(1)} %slice.52), channel_id=1, source_target_pairs={{0,1},{1,2},{2,3},{3,4},{4,5},{5,6},{6,7},{7,8},{8,9},{9,10},{10,1... | collective-permute-start | bytes 196616 | tf_op jit(solution)/shard_map/ppermute | solution.py:70
  33.9 0.1 slice.50
  34.0 1.2 %collective-permute-done.2 = bf16[4,1,4,2048]{3,2,1,0:T(4,128)(2,1)S(1)} collective-permute-done((bf16[4,1,4,2048]{3,2,1,0:T(4,128)(2,1)S(1)}, bf16[4,1,4,2048]{3,2,1,0:T(4,128)(2,1)S(1)}, u32[]{:S(2)}, u32[]{:S(2)}) %collective-permute-start.2) | collective-permute-done | bytes 65568 | tf_op jit(solution)/shard_map/ppermute | solution.py:70
  35.2 1.3 %copy_bitcast_fusion = bf16[4,8,4,16,128]{4,2,1,0,3:T(4,128)(2,1)} fusion(f32[4,7,4,2048]{3,2,1,0:T(4,128)S(1)} %slice.50, f32[4,1,4,2048]{3,2,1,0:T(4,128)S(1)} %convert_element_type.31, f32[4,8,4,2048]{3,2,1,0:T(4,128)S(1)} %get-tuple-element.6, pred[8]{0:T(512)(128)(4,1)S(1)} %add_compare_fusion, f32[8,4,2048]{2,1,0:T(4,128)S(1)} %copy-done.3), kind=kLoop, calls=%fused_computation.29 | loop fusion | flops 1572864 | bytes 2883592 | tf_op jit(solution)/shard_map/reshape | solution.py:75
  36.5 0.0 copy-start.10
  36.5 0.0 copy-start.11
  36.5 9.6 %all-to-all-start = ((bf16[4,8,4,16,128]{4,2,1,0,3:T(4,128)(2,1)}), bf16[4,8,4,16,128]{4,2,1,0,3:T(4,128)(2,1)S(1)}, u32[]{:S(2)}, u32[]{:S(2)}) async-start(bf16[4,8,4,16,128]{4,2,1,0,3:T(4,128)(2,1)} %copy_bitcast_fusion), calls=%async_computation | async-start | bytes 1048576 | tf_op jit(solution)/shard_map/all_to_all | solution.py:78
  46.1 0.0 copy-done.10
  46.2 0.0 copy-done.11
  46.2 0.1 pad_add_fusion
  46.2 0.1 fusion.19
  46.4 0.0 copy-start.7
  46.4 17.0 %all-to-all-done = bf16[4,8,4,16,128]{4,2,1,0,3:T(4,128)(2,1)S(1)} async-done(((bf16[4,8,4,16,128]{4,2,1,0,3:T(4,128)(2,1)}), bf16[4,8,4,16,128]{4,2,1,0,3:T(4,128)(2,1)S(1)}, u32[]{:S(2)}, u32[]{:S(2)}) %all-to-all-start) | async-done | bytes 524320 | tf_op jit(solution)/shard_map/all_to_all | solution.py:78
  63.4 0.0 copy-start.5
  63.4 0.1 copy.34
  63.5 0.1 copy.25
  63.6 0.0 copy-done.7
  63.6 0.9 %copy-done.5 = bf16[512,768]{1,0:T(8,128)(2,1)S(1)} copy-done((bf16[512,768]{1,0:T(8,128)(2,1)S(1)}, bf16[512,768]{1,0:T(8,128)(2,1)}, u32[]{:S(2)}) %copy-start.5) | copy-done | bytes 786456
  64.5 1.6 %fusion.3 = bf16[768,512]{0,1:T(8,128)(2,1)} fusion(bf16[512,512]{1,0:T(8,128)(2,1)S(1)} %bitcast.45, bf16[512,768]{1,0:T(8,128)(2,1)S(1)} %copy-done.5, f32[768]{0:T(1024)S(1)} %copy-done.7), kind=kOutput, calls=%fused_computation.5 | convolution fusion | flops 405012480 | bytes 2100224 | tf_op jit(solution)/shard_map/dot_general | solution.py:27
  66.1 0.0 copy-done
  66.1 0.0 copy-done.6
  66.1 0.0 copy-done.8
  66.1 0.0 copy-done.9
  66.1 3.3 %convolution_add_fusion.1 = f32[512,512]{1,0:T(8,128)} fusion(bf16[640,512]{1,0:T(8,128)(2,1)S(1)} %copy-done.6, bf16[768,512]{0,1:T(8,128)(2,1)} %fusion.3, bf16[768,640]{1,0:T(8,128)(2,1)S(1)} %copy-done, f32[640]{0:T(1024)S(1)} %copy-done.8, f32[512]{0:T(512)S(1)} %copy-done.9), kind=kOutput, calls=%fused_computation.8 | convolution fusion | flops 841089024 | bytes 3478016 | tf_op jit(solution)/shard_map/dot_general | solution.py:27
  69.4 1.5 %copy.26 = f32[512,4,128]{2,0,1:T(8,128)S(1)} copy(f32[512,4,128]{0,2,1:T(8,128)} %bitcast.44) | data formatting | bytes 2097152 | tf_op jit(solution)/shard_map/reshape | solution.py:88
  71.0 0.2 convert_add_fusion
  71.2 1.6 %copy.27 = f32[512,4,128]{2,1,0:T(4,128)} copy(f32[512,4,128]{2,0,1:T(8,128)S(1)} %convert_add_fusion) | data formatting | bytes 2097152 | tf_op jit(solution)/shard_map/add | solution.py:89
  (6 shorter events, 0.1 us)
Async XLA Ops:
  0.0 66.1 %copy-start = (bf16[768,640]{1,0:T(8,128)(2,1)S(1)}, bf16[768,640]{1,0:T(8,128)(2,1)}, u32[]{:S(2)}) copy-start(bf16[768,640]{1,0:T(8,128)(2,1)} %param.20) | copy-start | bytes 2949124
  0.0 19.4 %copy-start.1 = (f32[4,8,4,2048]{3,2,1,0:T(4,128)S(1)}, f32[4,8,4,2048]{3,2,1,0:T(4,128)}, u32[]{:S(2)}) copy-start(f32[4,8,4,2048]{3,2,1,0:T(4,128)} %param.12) | copy-start | bytes 3145732
  2.8 20.9 %collective-permute-start = (bf16[4,8,1,2048]{3,2,1,0:T(2,128)(2,1)}, bf16[4,8,1,2048]{3,2,1,0:T(2,128)(2,1)}, u32[]{:S(2)}, u32[]{:S(2)}) collective-permute-start(bf16[4,8,1,2048]{3,2,1,0:T(2,128)(2,1)} %get-tuple-element.13), channel_id=1, source_target_pairs={{0,16},{16,32},{32,48},{48,64},{64,80},{80,96},{96,112},{112,128},... | collective-permute-start | bytes 393224 | tf_op jit(solution)/shard_map/ppermute | solution.py:14
  6.8 14.3 %copy-start.4 = (f32[8,4,2048]{2,1,0:T(4,128)S(1)}, f32[8,4,2048]{2,1,0:T(4,128)}, u32[]{:S(2)}) copy-start(f32[8,4,2048]{2,1,0:T(4,128)} %param.14) | copy-start | bytes 786436
  6.8 18.1 %collective-permute-start.1 = (bf16[4,8,1,2048]{3,2,1,0:T(2,128)(2,1)}, bf16[4,8,1,2048]{3,2,1,0:T(2,128)(2,1)}, u32[]{:S(2)}, u32[]{:S(2)}) collective-permute-start(bf16[4,8,1,2048]{3,2,1,0:T(2,128)(2,1)} %get-tuple-element.14), channel_id=1, source_target_pairs={{16,0},{32,16},{48,32},{64,48},{80,64},{96,80},{112,96},{128,112},... | collective-permute-start | bytes 393224 | tf_op jit(solution)/shard_map/ppermute | solution.py:15
  23.2 2.9 %copy-start.3 = (f32[8,4,2048]{2,1,0:T(4,128)S(1)}, f32[8,4,2048]{2,1,0:T(4,128)}, u32[]{:S(2)}) copy-start(f32[8,4,2048]{2,1,0:T(4,128)} %param.15) | copy-start | bytes 786436
  23.2 2.9 %copy-start.2 = (f32[4,8,4,2047]{3,2,1,0:T(4,128)S(1)}, f32[4,8,4,2047]{3,2,1,0:T(4,128)}, u32[]{:S(2)}) copy-start(f32[4,8,4,2047]{3,2,1,0:T(4,128)} %get-tuple-element.10) | copy-start | bytes 3144196
  29.5 5.7 %collective-permute-start.2 = (bf16[4,1,4,2048]{3,2,1,0:T(4,128)(2,1)S(1)}, bf16[4,1,4,2048]{3,2,1,0:T(4,128)(2,1)S(1)}, u32[]{:S(2)}, u32[]{:S(2)}) collective-permute-start(bf16[4,1,4,2048]{3,2,1,0:T(4,128)(2,1)S(1)} %slice.52), channel_id=1, source_target_pairs={{0,1},{1,2},{2,3},{3,4},{4,5},{5,6},{6,7},{7,8},{8,9},{9,10},{10,1... | collective-permute-start | bytes 196616 | tf_op jit(solution)/shard_map/ppermute | solution.py:70
  36.5 9.6 %copy-start.10 = (s32[1,1,2]{2,1,0:T(1,128)S(1)}, s32[1,1,2]{2,1,0:T(1,128)}, u32[]{:S(2)}) copy-start(s32[1,1,2]{2,1,0:T(1,128)} %param.17) | copy-start | bytes 28
  36.5 9.6 %copy-start.11 = (s32[1,1,2]{2,1,0:T(1,128)S(1)}, s32[1,1,2]{2,1,0:T(1,128)}, u32[]{:S(2)}) copy-start(s32[1,1,2]{2,1,0:T(1,128)} %param.16) | copy-start | bytes 28
  36.5 26.8 %all-to-all-start = ((bf16[4,8,4,16,128]{4,2,1,0,3:T(4,128)(2,1)}), bf16[4,8,4,16,128]{4,2,1,0,3:T(4,128)(2,1)S(1)}, u32[]{:S(2)}, u32[]{:S(2)}) async-start(bf16[4,8,4,16,128]{4,2,1,0,3:T(4,128)(2,1)} %copy_bitcast_fusion), calls=%async_computation | async-start | bytes 1048576 | tf_op jit(solution)/shard_map/all_to_all | solution.py:78
  46.4 17.2 %copy-start.7 = (f32[768]{0:T(1024)S(1)}, f32[768]{0:T(1024)}, u32[]{:S(2)}) copy-start(f32[768]{0:T(1024)} %param.19) | copy-start | bytes 9220
  63.4 1.1 %copy-start.5 = (bf16[512,768]{1,0:T(8,128)(2,1)S(1)}, bf16[512,768]{1,0:T(8,128)(2,1)}, u32[]{:S(2)}) copy-start(bf16[512,768]{1,0:T(8,128)(2,1)} %param.18) | copy-start | bytes 2359300
  64.5 1.7 %copy-start.6 = (bf16[640,512]{1,0:T(8,128)(2,1)S(1)}, bf16[640,512]{1,0:T(8,128)(2,1)}, u32[]{:S(2)}) copy-start(bf16[640,512]{1,0:T(8,128)(2,1)} %param.22) | copy-start | bytes 1966084
  64.5 1.7 %copy-start.8 = (f32[640]{0:T(1024)S(1)}, f32[640]{0:T(1024)}, u32[]{:S(2)}) copy-start(f32[640]{0:T(1024)} %param.21) | copy-start | bytes 7684
  64.5 1.7 %copy-start.9 = (f32[512]{0:T(512)S(1)}, f32[512]{0:T(512)}, u32[]{:S(2)}) copy-start(f32[512]{0:T(512)} %param.23) | copy-start | bytes 6148

commit v2 on v1

v2 whole, which is shorter than its diff:
```python
import jax
import jax.numpy as jnp
from jax import lax
from jax.experimental import pallas as pl
from jax.experimental.pallas import tpu as pltpu
from jax.sharding import PartitionSpec as P

MESH = pl.DeviceIdType.MESH
PAIRS = ((1, 2), (0, 3))


def silu(value):
    return value * (0.5 + 0.5 * jnp.tanh(0.5 * value))


def kernel(
    fields_hbm,
    lon_hbm,
    lat_hbm,
    move_hbm,
    own_hbm,
    lent_hbm,
    w1_hbm,
    b1_hbm,
    w2_hbm,
    b2_hbm,
    w3_hbm,
    b3_hbm,
    out_hbm,
    fb,
    cb,
    part,
    halo_out,
    halo_in,
    flux_out,
    flux_in,
    send,
    recv,
    w1,
    w2,
    w3,
    w1t,
    w2t,
    w3t,
    b1,
    b2,
    b3,
    ob,
    h1,
    h2,
    own_ref,
    lent_ref,
    b1_line,
    b2_line,
    b3_line,
    field_sem,
    wind_sem,
    weight_sem,
    out_sem,
    halo_send_sem,
    halo_recv_sem,
    flux_send_sem,
    flux_recv_sem,
    send_sem,
    recv_sem,
):
    count = lax.axis_size("lev")
    bands = lax.axis_size("lat")
    lev = lax.axis_index("lev")
    lat = lax.axis_index("lat")
    north, south = lax.rem(lat + bands - 1, bands), lax.rem(lat + 1, bands)
    nfield, nrow, nlev, lon = fb.shape

    field_copies = {}
    wind_copies = {}
    for r in (0, 3, 1, 2):
        field_copies[r] = pltpu.make_async_copy(
            fields_hbm.at[:, :, r, :], fb.at[:, r], field_sem.at[r]
        )
        field_copies[r].start()
    for r in (1, 2, 0, 3):
        for i, src in enumerate((lon_hbm, lat_hbm, move_hbm)):
            wind_copies[i, r] = pltpu.make_async_copy(
                src.at[:, r, :], cb.at[i, r], wind_sem.at[i, r]
            )
            wind_copies[i, r].start()
    weight_copies = []
    moves = (
        (w1_hbm, w1),
        (b1_hbm, b1_line),
        (b2_hbm, b2_line),
        (b3_hbm, b3_line),
        (own_hbm, own_ref),
        (lent_hbm, lent_ref),
        (w2_hbm, w2),
        (w3_hbm, w3),
    )
    for i, (src, dst) in enumerate(moves):
        weight_copies.append(pltpu.make_async_copy(src, dst, weight_sem.at[i]))
        weight_copies[i].start()

    barrier = pltpu.get_barrier_semaphore()
    for off in range(1, count):
        pl.semaphore_signal(
            barrier, 1, device_id={"lev": lax.rem(lev + off, count)}, device_id_type=MESH
        )
    for other in (north, south):
        pl.semaphore_signal(barrier, 1, device_id={"lat": other}, device_id_type=MESH)

    sub = lax.broadcasted_iota(jnp.int32, (nlev, lon), 0)

    def advect(r, k):
        lonp = jnp.maximum(cb[0, r], 0.0)
        lonn = jnp.minimum(cb[0, r], 0.0)
        latp = jnp.maximum(cb[1, r], 0.0)
        latn = jnp.minimum(cb[1, r], 0.0)
        move = cb[2, r]
        last = jnp.logical_and(sub == nlev - 1, lev == count - 1)
        move = jnp.where(last, 0.0, move)
        for f in range(nfield):
            x = fb[f, r]
            half = pl.ds((f % 2) * nlev, nlev)
            if r == 0:
                up = halo_in[0, f // 2].astype(jnp.float32)
                up = up[(f % 2) * nlev : (f % 2 + 1) * nlev]
                up = jnp.where(lat == 0, 0.0, up)
            else:
                up = fb[f, r - 1]
            if r == nrow - 1:
                down = halo_in[1, f // 2].astype(jnp.float32)
                down = down[(f % 2) * nlev : (f % 2 + 1) * nlev]
                down = jnp.where(lat == bands - 1, 0.0, down)
            else:
                down = fb[f, r + 1]
            value = x - lonp * (x - pltpu.roll(x, 1, 1))
            value = value - lonn * (pltpu.roll(x, lon - 1, 1) - x)
            value = value - latp * (x - up)
            value = value - latn * (down - x)
            flux = move * value
            turned = pltpu.roll(flux, 1, 0)
            part[f, r] = value - flux + jnp.where(sub == 0, 0.0, turned)
            flux_out[k // 4, (k % 4) * nfield + f : (k % 4) * nfield + f + 1, :] = turned[0:1]

    def flux_copy(p):
        return pltpu.make_async_remote_copy(
            src_ref=flux_out.at[p],
            dst_ref=flux_in.at[p],
            send_sem=flux_send_sem.at[p],
            recv_sem=flux_recv_sem.at[p],
            device_id={"lev": lax.rem(lev + 1, count)},
            device_id_type=MESH,
        )

    def halo_copy(i):
        return pltpu.make_async_remote_copy(
            src_ref=halo_out.at[i],
            dst_ref=halo_in.at[i],
            send_sem=halo_send_sem.at[i],
            recv_sem=halo_recv_sem.at[i],
            device_id={"lat": south if i == 0 else north},
            device_id_type=MESH,
        )

    def block_copy(p, off):
        target = lax.rem(lev + off, count)
        return pltpu.make_async_remote_copy(
            src_ref=send.at[p, target],
            dst_ref=recv.at[p, lev],
            send_sem=send_sem.at[p, off - 1],
            recv_sem=recv_sem.at[p, off - 1],
            device_id={"lev": target},
            device_id_type=MESH,
        )

    def finish(p):
        for i, r in enumerate(PAIRS[p]):
            for pair in range(nfield // 2):
                values = []
                for f in (2 * pair, 2 * pair + 1):
                    enter = flux_in[p, i * nfield + f : i * nfield + f + 1, :]
                    enter = jnp.broadcast_to(enter, (nlev, lon))
                    values.append(part[f, r] + jnp.where(sub == 0, enter, 0.0))
                both = jnp.concatenate(values, axis=0).astype(jnp.bfloat16)
                row = i * nfield * nlev + pair * 2 * nlev
                for g in range(16):
                    send[p, g, row : row + 2 * nlev, :] = both[:, g * 128 : (g + 1) * 128]
        for off in ORDER:
            block_copy(p, off).start()

    field_copies[0].wait()
    field_copies[3].wait()
    for i, r in ((0, 3), (1, 0)):
        for pair in range(nfield // 2):
            both = jnp.concatenate([fb[2 * pair, r], fb[2 * pair + 1, r]], axis=0)
            halo_out[i, pair] = both.astype(jnp.bfloat16)
    field_copies[1].wait()
    field_copies[2].wait()
    for k, r in enumerate(PAIRS[0]):
        for i in range(3):
            wind_copies[i, r].wait()
        advect(r, k)

    pl.semaphore_wait(barrier, count + 1)
    flux_copy(0).start()
    for i in range(2):
        halo_copy(i).start()

    for copy in weight_copies:
        copy.wait()
    w1t[...] = w1[...].T

    flux_copy(0).wait_recv()
    finish(0)

    for r in PAIRS[1]:
        for i in range(3):
            wind_copies[i, r].wait()
    for i in range(2):
        halo_copy(i).wait_recv()
    for k, r in enumerate(PAIRS[1]):
        advect(r, 4 + k)
    flux_copy(1).start()
    w2t[...] = w2[...].T
    flux_copy(1).wait_recv()
    finish(1)

    w3t[...] = w3[...].T
    for src, dst in ((b1_line, b1), (b2_line, b2), (b3_line, b3)):
        for i in range(dst.shape[0] // 128):
            line = jnp.broadcast_to(src[i * 128 : (i + 1) * 128][None], (128, 128))
            dst[i * 128 : (i + 1) * 128, :] = line.T

    def unpack(p, block, source):
        for i, r in enumerate(PAIRS[p]):
            for f in range(nfield):
                row = i * nfield * nlev + f * nlev
                start = pl.multiple_of(f * nlev * count + source * nlev, 8)
                ob[r, pl.ds(start, nlev), :] = block[row : row + nlev]

    def twice(value):
        return jnp.concatenate([value, value], axis=1)

    def physics(p):
        ra, rb = PAIRS[p]
        x = jnp.concatenate([ob[ra], ob[rb]], axis=1).astype(jnp.bfloat16)
        for start in range(0, 768, 256):
            rows = slice(start, start + 256)
            v = jnp.dot(w1t[rows], x, preferred_element_type=jnp.float32)
            h1[rows] = silu(v + twice(b1[rows])).astype(jnp.bfloat16)
        x = h1[...]
        for start in range(0, 640, 128):
            rows = slice(start, start + 128)
            v = jnp.dot(w2t[rows], x, preferred_element_type=jnp.float32)
            h2[rows] = silu(v + twice(b2[rows])).astype(jnp.bfloat16)
        x = h2[...]
        active = []
        for r in (ra, rb):
            hit = own_ref[0, 0, 0] == r
            for other in (own_ref[0, 0, 1], lent_ref[0, 0, 0], lent_ref[0, 0, 1]):
                hit = jnp.logical_or(hit, other == r)
            active.append(hit)
        for start in range(0, 512, 256):
            rows = slice(start, start + 256)
            v = jnp.dot(w3t[rows], x, preferred_element_type=jnp.float32)
            v = (v + twice(b3[rows])).astype(jnp.bfloat16).astype(jnp.float32)
            for i, r in enumerate((ra, rb)):
                ob[r, rows] = ob[r, rows] + jnp.where(
                    active[i], v[:, i * 128 : (i + 1) * 128], 0.0
                )
        for r in (ra, rb):
            out_copy(r).start()

    def out_copy(r):
        return pltpu.make_async_copy(ob.at[r], out_hbm.at[:, r, :], out_sem.at[r])

    for p in range(2):
        unpack(p, send[p, lev].astype(jnp.float32), lev)
        for off in ORDER:
            block_copy(p, off).wait_recv()
            source = lax.rem(lev + count - off, count)
            unpack(p, recv[p, source].astype(jnp.float32), source)
        physics(p)

    for p in range(2):
        flux_copy(p).wait_send()
        halo_copy(p).wait_send()
        for off in ORDER:
            block_copy(p, off).wait_send()
    for r in range(nrow):
        out_copy(r).wait()


ORDER = (8, 7, 9, 6, 10, 5, 11, 4, 12, 3, 13, 2, 14, 1, 15)


def in_hbm(value):
    return pltpu.with_memory_space_constraint(value, pltpu.HBM)


def body(
    fields,
    courant_lon,
    courant_lat,
    displacement,
    own_slot,
    lent_slot,
    w_first,
    bias_first,
    w_second,
    bias_second,
    w_third,
    bias_third,
):
    nfield, nlev, nrow, lon = fields.shape
    count = lax.axis_size("lev")
    width = nfield * nlev * count
    part = lon // count
    hidden = (w_first.shape[1], w_second.shape[1])
    f32, bf16 = jnp.float32, jnp.bfloat16
    hbm = pl.BlockSpec(memory_space=pltpu.HBM)
    dma = pltpu.SemaphoreType.DMA
    return pl.pallas_call(
        kernel,
        name="tracer",
        out_shape=jax.ShapeDtypeStruct((width, nrow, part), f32),
        in_specs=[hbm] * 12,
        out_specs=pl.BlockSpec(memory_space=pl.ANY),
        scratch_shapes=[
            pltpu.VMEM((nfield, nrow, nlev, lon), f32),
            pltpu.VMEM((3, nrow, nlev, lon), f32),
            pltpu.VMEM((nfield, nrow, nlev, lon), f32),
            pltpu.VMEM((2, nfield // 2, 2 * nlev, lon), bf16),
            pltpu.VMEM((2, nfield // 2, 2 * nlev, lon), bf16),
            pltpu.VMEM((2, 2 * nfield, lon), f32),
            pltpu.VMEM((2, 2 * nfield, lon), f32),
            pltpu.VMEM((2, count, 2 * nfield * nlev, part), bf16),
            pltpu.VMEM((2, count, 2 * nfield * nlev, part), bf16),
            pltpu.VMEM((width, hidden[0]), bf16),
            pltpu.VMEM((hidden[0], hidden[1]), bf16),
            pltpu.VMEM((hidden[1], width), bf16),
            pltpu.VMEM((hidden[0], width), bf16),
            pltpu.VMEM((hidden[1], hidden[0]), bf16),
            pltpu.VMEM((width, hidden[1]), bf16),
            pltpu.VMEM((hidden[0], 128), f32),
            pltpu.VMEM((hidden[1], 128), f32),
            pltpu.VMEM((width, 128), f32),
            pltpu.VMEM((nrow, width, part), f32),
            pltpu.VMEM((hidden[0], 2 * part), bf16),
            pltpu.VMEM((hidden[1], 2 * part), bf16),
            pltpu.SMEM(own_slot.shape, jnp.int32),
            pltpu.SMEM(lent_slot.shape, jnp.int32),
            pltpu.VMEM(bias_first.shape, f32),
            pltpu.VMEM(bias_second.shape, f32),
            pltpu.VMEM(bias_third.shape, f32),
            dma((nrow,)),
            dma((3, nrow)),
            dma((8,)),
            dma((nrow,)),
            dma((2,)),
            dma((2,)),
            dma((2,)),
            dma((2,)),
            dma((2, count - 1)),
            dma((2, count - 1)),
        ],
        compiler_params=pltpu.CompilerParams(
            collective_id=0, has_side_effects=True, vmem_limit_bytes=48 << 20
        ),
    )(
        in_hbm(fields),
        in_hbm(courant_lon),
        in_hbm(courant_lat),
        in_hbm(displacement),
        in_hbm(own_slot),
        in_hbm(lent_slot),
        in_hbm(w_first),
        in_hbm(bias_first),
        in_hbm(w_second),
        in_hbm(bias_second),
        in_hbm(w_third),
        in_hbm(bias_third),
    )


def solution(mesh):
    in_specs = (
        P(None, "lev", "lat", None),
        P("lev", "lat", None),
        P("lev", "lat", None),
        P("lev", "lat", None),
        P("lev", "lat", None),
        P("lev", "lat", None),
        P(),
        P(),
        P(),
        P(),
        P(),
        P(),
    )
    out_specs = P(None, "lat", "lev")
    return jax.shard_map(body, mesh=mesh, in_specs=in_specs, out_specs=out_specs, check_vma=False)
```

time: 73.3 us -> 38.8 us (0.53)
  the two profiles are of different devices: /device:TPU:7 before, /device:TPU:1 now
where the time goes in v2:
time: 38.8 us; the launch traced here: 38.7 us
  Pallas kernels  37.7 us (97%)
  local copies, waits for them, and re-layouts  0.97 us (2%)
    pallas_call x1, Pallas kernels, body(): pl.pallas_call(kernel, name='tracer', out_shape=jax.ShapeDtypeStruct((wid...  37.7 us
    unnamed x1, local copies, waits for them, and re-layouts  0.97 us

profile of v2, /device:TPU:1, one launch (start us, length us, event | category | flops | bytes accessed | tf_op | source)
XLA Modules:
  0.0 38.7 jit_solution(3104207922991044605)
XLA Ops:
  0.0 37.7 %tracer.1 = f32[512,4,128]{2,1,0:T(4,128)S(1)} custom-call(f32[4,8,4,2048]{3,2,1,0:T(4,128)} %fields_hbm.1, f32[8,4,2048]{2,1,0:T(4,128)} %lon_hbm.1, f32[8,4,2048]{2,1,0:T(4,128)} %lat_hbm.1, f32[8,4,2048]{2,1,0:T(4,128)} %move_hbm.1, s32[1,1,2]{2,1,0:T(1,128)} %own_hbm.1, s32[1,1,2]{2,1,0:T(1,128)} %lent_hbm.1, bf16[512,768]{1,0:T(8,128)(2,1)} %w1_hbm.1, ...), custom_call_target="tpu_custom_call" | custom-call | tf_op jit(solution)/shard_map/tracer/pallas_call | solution.py:322
  37.8 1.0 %copy.14 = f32[512,4,128]{2,1,0:T(4,128)} copy(f32[512,4,128]{2,1,0:T(4,128)S(1)} %tracer.1) | data formatting | bytes 2097152

commit v3 on v2

--- a/solution.py
+++ b/solution.py
@@ -26,12 +26,13 @@
     b2_hbm,
     w3_hbm,
     b3_hbm,
-    out_hbm,
+    out,
     fb,
     cb,
     part,
     halo_out,
     halo_in,
+    flux_row,
     flux_out,
     flux_in,
     send,
@@ -46,6 +47,7 @@
     b2,
     b3,
     ob,
+    x_buf,
     h1,
     h2,
     own_ref,
@@ -56,7 +58,6 @@
     field_sem,
     wind_sem,
     weight_sem,
-    out_sem,
     halo_send_sem,
     halo_recv_sem,
     flux_send_sem,
@@ -97,7 +98,6 @@
     )
     for i, (src, dst) in enumerate(moves):
         weight_copies.append(pltpu.make_async_copy(src, dst, weight_sem.at[i]))
-        weight_copies[i].start()
 
     barrier = pltpu.get_barrier_semaphore()
     for off in range(1, count):
@@ -139,15 +139,16 @@
             flux = move * value
             turned = pltpu.roll(flux, 1, 0)
             part[f, r] = value - flux + jnp.where(sub == 0, 0.0, turned)
-            flux_out[k // 4, (k % 4) * nfield + f : (k % 4) * nfield + f + 1, :] = turned[0:1]
-
-    def flux_copy(p):
+            flux_row[k * nfield + f : k * nfield + f + 1, :] = turned[0:1]
+
+    def flux_copy(p, off):
+        target = lax.rem(lev + off, count)
         return pltpu.make_async_remote_copy(
-            src_ref=flux_out.at[p],
-            dst_ref=flux_in.at[p],
-            send_sem=flux_send_sem.at[p],
-            recv_sem=flux_recv_sem.at[p],
-            device_id={"lev": lax.rem(lev + 1, count)},
+            src_ref=flux_out.at[p, target],
+            dst_ref=flux_in.at[p, lev],
+            send_sem=flux_send_sem.at[p, off - 1],
+            recv_sem=flux_recv_sem.at[p, off - 1],
+            device_id={"lev": target},
             device_id_type=MESH,
         )
 
@@ -175,17 +176,19 @@
     def finish(p):
         for i, r in enumerate(PAIRS[p]):
             for pair in range(nfield // 2):
-                values = []
-                for f in (2 * pair, 2 * pair + 1):
-                    enter = flux_in[p, i * nfield + f : i * nfield + f + 1, :]
-                    enter = jnp.broadcast_to(enter, (nlev, lon))
-                    values.append(part[f, r] + jnp.where(sub == 0, enter, 0.0))
-                both = jnp.concatenate(values, axis=0).astype(jnp.bfloat16)
+                both = jnp.concatenate([part[2 * pair, r], part[2 * pair + 1, r]], axis=0)
+                both = both.astype(jnp.bfloat16)
                 row = i * nfield * nlev + pair * 2 * nlev
                 for g in range(16):
                     send[p, g, row : row + 2 * nlev, :] = both[:, g * 128 : (g + 1) * 128]
+        edge = flux_row[...].astype(jnp.bfloat16)
+        for g in range(16):
+            flux_out[p, g] = edge[:, g * 128 : (g + 1) * 128]
         for off in ORDER:
+            flux_copy(p, off).start()
             block_copy(p, off).start()
+        recv[p, lev] = send[p, lev]
+        flux_in[p, lev] = flux_out[p, lev]
 
     field_copies[0].wait()
     field_copies[3].wait()
@@ -199,17 +202,12 @@
         for i in range(3):
             wind_copies[i, r].wait()
         advect(r, k)
+    for copy in weight_copies:
+        copy.start()
 
     pl.semaphore_wait(barrier, count + 1)
-    flux_copy(0).start()
     for i in range(2):
         halo_copy(i).start()
-
-    for copy in weight_copies:
-        copy.wait()
-    w1t[...] = w1[...].T
-
-    flux_copy(0).wait_recv()
     finish(0)
 
     for r in PAIRS[1]:
@@ -218,31 +216,53 @@
     for i in range(2):
         halo_copy(i).wait_recv()
     for k, r in enumerate(PAIRS[1]):
-        advect(r, 4 + k)
-    flux_copy(1).start()
+        advect(r, k)
+    finish(1)
+
+    for copy in weight_copies:
+        copy.wait()
+    w1t[...] = w1[...].T
     w2t[...] = w2[...].T
-    flux_copy(1).wait_recv()
-    finish(1)
-
     w3t[...] = w3[...].T
     for src, dst in ((b1_line, b1), (b2_line, b2), (b3_line, b3)):
         for i in range(dst.shape[0] // 128):
             line = jnp.broadcast_to(src[i * 128 : (i + 1) * 128][None], (128, 128))
             dst[i * 128 : (i + 1) * 128, :] = line.T
 
-    def unpack(p, block, source):
+    top = lax.broadcasted_iota(jnp.int32, (nlev, 128), 0) == 0
+
+    def unpack(p):
+        for off in ORDER:
+            flux_copy(p, off).wait_recv()
+            block_copy(p, off).wait_recv()
         for i, r in enumerate(PAIRS[p]):
-            for f in range(nfield):
-                row = i * nfield * nlev + f * nlev
-                start = pl.multiple_of(f * nlev * count + source * nlev, 8)
-                ob[r, pl.ds(start, nlev), :] = block[row : row + nlev]
+            for pair in range(nfield // 2):
+                pieces = ([], [])
+                for g in range(16):
+                    row = i * nfield * nlev + pair * 2 * nlev
+                    both = recv[p, g, row : row + 2 * nlev].astype(jnp.float32)
+                    for j in range(2):
+                        piece = both[j * nlev : (j + 1) * nlev]
+                        if g > 0:
+                            k = i * nfield + 2 * pair + j
+                            edge = flux_in[p, g - 1].astype(jnp.float32)[k : k + 1]
+                            edge = jnp.broadcast_to(edge, (nlev, 128))
+                            piece = piece + jnp.where(top, edge, 0.0)
+                        pieces[j].append(piece)
+                for j in range(2):
+                    f = 2 * pair + j
+                    whole = jnp.concatenate(pieces[j], axis=0)
+                    ob[r, f * 128 : (f + 1) * 128] = whole
+                    x_buf[f * 128 : (f + 1) * 128, i * 128 : (i + 1) * 128] = whole.astype(
+                        jnp.bfloat16
+                    )
 
     def twice(value):
         return jnp.concatenate([value, value], axis=1)
 
     def physics(p):
         ra, rb = PAIRS[p]
-        x = jnp.concatenate([ob[ra], ob[rb]], axis=1).astype(jnp.bfloat16)
+        x = x_buf[...]
         for start in range(0, 768, 256):
             rows = slice(start, start + 256)
             v = jnp.dot(w1t[rows], x, preferred_element_type=jnp.float32)
@@ -264,30 +284,19 @@
             v = jnp.dot(w3t[rows], x, preferred_element_type=jnp.float32)
             v = (v + twice(b3[rows])).astype(jnp.bfloat16).astype(jnp.float32)
             for i, r in enumerate((ra, rb)):
-                ob[r, rows] = ob[r, rows] + jnp.where(
+                out[pl.ds(start * nrow + r, 256, stride=nrow), :] = ob[r, rows] + jnp.where(
                     active[i], v[:, i * 128 : (i + 1) * 128], 0.0
                 )
-        for r in (ra, rb):
-            out_copy(r).start()
-
-    def out_copy(r):
-        return pltpu.make_async_copy(ob.at[r], out_hbm.at[:, r, :], out_sem.at[r])
 
     for p in range(2):
-        unpack(p, send[p, lev].astype(jnp.float32), lev)
-        for off in ORDER:
-            block_copy(p, off).wait_recv()
-            source = lax.rem(lev + count - off, count)
-            unpack(p, recv[p, source].astype(jnp.float32), source)
+        unpack(p)
         physics(p)
 
     for p in range(2):
-        flux_copy(p).wait_send()
         halo_copy(p).wait_send()
         for off in ORDER:
+            flux_copy(p, off).wait_send()
             block_copy(p, off).wait_send()
-    for r in range(nrow):
-        out_copy(r).wait()
 
 
 ORDER = (8, 7, 9, 6, 10, 5, 11, 4, 12, 3, 13, 2, 14, 1, 15)
@@ -322,17 +331,18 @@
     return pl.pallas_call(
         kernel,
         name="tracer",
-        out_shape=jax.ShapeDtypeStruct((width, nrow, part), f32),
+        out_shape=jax.ShapeDtypeStruct((width * nrow, part), f32),
         in_specs=[hbm] * 12,
-        out_specs=pl.BlockSpec(memory_space=pl.ANY),
+        out_specs=pl.BlockSpec(memory_space=pltpu.VMEM),
         scratch_shapes=[
             pltpu.VMEM((nfield, nrow, nlev, lon), f32),
             pltpu.VMEM((3, nrow, nlev, lon), f32),
             pltpu.VMEM((nfield, nrow, nlev, lon), f32),
             pltpu.VMEM((2, nfield // 2, 2 * nlev, lon), bf16),
             pltpu.VMEM((2, nfield // 2, 2 * nlev, lon), bf16),
-            pltpu.VMEM((2, 2 * nfield, lon), f32),
-            pltpu.VMEM((2, 2 * nfield, lon), f32),
+            pltpu.VMEM((2 * nfield, lon), f32),
+            pltpu.VMEM((2, count, 2 * nfield, part), bf16),
+            pltpu.VMEM((2, count, 2 * nfield, part), bf16),
             pltpu.VMEM((2, count, 2 * nfield * nlev, part), bf16),
             pltpu.VMEM((2, count, 2 * nfield * nlev, part), bf16),
             pltpu.VMEM((width, hidden[0]), bf16),
@@ -345,6 +355,7 @@
             pltpu.VMEM((hidden[1], 128), f32),
             pltpu.VMEM((width, 128), f32),
             pltpu.VMEM((nrow, width, part), f32),
+            pltpu.VMEM((width, 2 * part), bf16),
             pltpu.VMEM((hidden[0], 2 * part), bf16),
             pltpu.VMEM((hidden[1], 2 * part), bf16),
             pltpu.SMEM(own_slot.shape, jnp.int32),
@@ -355,11 +366,10 @@
             dma((nrow,)),
             dma((3, nrow)),
             dma((8,)),
-            dma((nrow,)),
             dma((2,)),
             dma((2,)),
-            dma((2,)),
-            dma((2,)),
+            dma((2, count - 1)),
+            dma((2, count - 1)),
             dma((2, count - 1)),
             dma((2, count - 1)),
         ],
@@ -379,7 +389,7 @@
         in_hbm(bias_second),
         in_hbm(w_third),
         in_hbm(bias_third),
-    )
+    ).reshape(width, nrow, part)
 
 
 def solution(mesh):

time: 38.8 us -> 38 us (0.979)
  Pallas kernels: 37.7 us -> 36.8 us
    pallas_call x1, Pallas kernels: 37.7 us -> 36.8 us  [body(): pl.pallas_call(kernel, name='tracer', out_shape=jax.ShapeDtypeStruct((wid...]
where the time goes in v3:
time: 38 us; the launch traced here: 37.8 us
  Pallas kernels  36.8 us (97%)
  local copies, waits for them, and re-layouts  0.97 us (3%)
    pallas_call x1, Pallas kernels, body(): pl.pallas_call(kernel, name='tracer', out_shape=jax.ShapeDtypeStruct((wid...  36.8 us
    unnamed x1, local copies, waits for them, and re-layouts  0.97 us

profile of v3, /device:TPU:1, one launch (start us, length us, event | category | flops | bytes accessed | tf_op | source)
XLA Modules:
  0.0 37.8 jit_solution(16966903861759082130)
XLA Ops:
  0.0 36.8 %tracer.1 = f32[2048,128]{1,0:T(8,128)S(1)} custom-call(f32[4,8,4,2048]{3,2,1,0:T(4,128)} %fields_hbm.1, f32[8,4,2048]{2,1,0:T(4,128)} %lon_hbm.1, f32[8,4,2048]{2,1,0:T(4,128)} %lat_hbm.1, f32[8,4,2048]{2,1,0:T(4,128)} %move_hbm.1, s32[1,1,2]{2,1,0:T(1,128)} %own_hbm.1, s32[1,1,2]{2,1,0:T(1,128)} %lent_hbm.1, bf16[512,768]{1,0:T(8,128)(2,1)} %w1_hbm.1, ...), custom_call_target="tpu_custom_call" | custom-call | tf_op jit(solution)/shard_map/tracer/pallas_call | solution.py:331
  36.9 1.0 %copy.14 = f32[512,4,128]{2,1,0:T(4,128)} copy(f32[512,4,128]{2,1,0:T(4,128)S(1)} %bitcast.1) | data formatting | bytes 2097152

commit v4 on v3

--- a/solution.py
+++ b/solution.py
@@ -6,7 +6,7 @@
 from jax.sharding import PartitionSpec as P
 
 MESH = pl.DeviceIdType.MESH
-PAIRS = ((1, 2), (0, 3))
+STAGES = ((1, 2), (3,), (0,))
 
 
 def silu(value):
@@ -33,38 +33,41 @@
     halo_out,
     halo_in,
     flux_row,
-    flux_out,
-    flux_in,
-    send,
-    recv,
-    w1,
-    w2,
-    w3,
-    w1t,
-    w2t,
-    w3t,
-    b1,
-    b2,
-    b3,
-    ob,
-    x_buf,
-    h1,
-    h2,
-    own_ref,
-    lent_ref,
-    b1_line,
-    b2_line,
-    b3_line,
-    field_sem,
-    wind_sem,
-    weight_sem,
-    halo_send_sem,
-    halo_recv_sem,
-    flux_send_sem,
-    flux_recv_sem,
-    send_sem,
-    recv_sem,
+    *refs,
 ):
+    buffers, refs = refs[: 4 * len(STAGES)], refs[4 * len(STAGES) :]
+    flux_out, flux_in, send, recv = (buffers[k :: 4] for k in range(4))
+    (
+        w1,
+        w2,
+        w3,
+        w1t,
+        w2t,
+        w3t,
+        b1,
+        b2,
+        b3,
+        ob,
+        x_buf,
+        h1,
+        h2,
+        own_ref,
+        lent_ref,
+        b1_line,
+        b2_line,
+        b3_line,
+        field_sem,
+        wind_sem,
+        weight_sem,
+        halo_send_sem,
+        halo_recv_sem,
+        ready_lat,
+        ready_lev,
+        flux_send_sem,
+        flux_recv_sem,
+        send_sem,
+        recv_sem,
+    ) = refs
     count = lax.axis_size("lev")
     bands = lax.axis_size("lat")
     lev = lax.axis_index("lev")
@@ -99,13 +102,30 @@
     for i, (src, dst) in enumerate(moves):
         weight_copies.append(pltpu.make_async_copy(src, dst, weight_sem.at[i]))
 
+    first_band = lat == 0
+    last_band = lat == bands - 1
+    late_owner = jnp.logical_and(first_band, lev == 0)
+    late_peer = jnp.logical_and(first_band, lev != 0)
+
     barrier = pltpu.get_barrier_semaphore()
-    for off in range(1, count):
-        pl.semaphore_signal(
-            barrier, 1, device_id={"lev": lax.rem(lev + off, count)}, device_id_type=MESH
-        )
-    for other in (north, south):
-        pl.semaphore_signal(barrier, 1, device_id={"lat": other}, device_id_type=MESH)
+
+    @pl.when(jnp.logical_not(late_owner))
+    def _():
+        for off in ORDER:
+            target = lax.rem(lev + off, count)
+            pl.semaphore_signal(barrier, 1, device_id={"lev": target}, device_id_type=MESH)
+
+    @pl.when(jnp.logical_not(first_band))
+    def _():
+        pl.semaphore_signal(barrier, 1, device_id={"lat": north}, device_id_type=MESH)
+
+    @pl.when(first_band)
+    def _():
+        halo_in[0] = jnp.zeros(halo_in.shape[1:], halo_in.dtype)
+
+    @pl.when(last_band)
+    def _():
+        halo_in[1] = jnp.zeros(halo_in.shape[1:], halo_in.dtype)
 
     sub = lax.broadcasted_iota(jnp.int32, (nlev, lon), 0)
 
@@ -119,17 +139,14 @@
         move = jnp.where(last, 0.0, move)
         for f in range(nfield):
             x = fb[f, r]
-            half = pl.ds((f % 2) * nlev, nlev)
             if r == 0:
                 up = halo_in[0, f // 2].astype(jnp.float32)
                 up = up[(f % 2) * nlev : (f % 2 + 1) * nlev]
-                up = jnp.where(lat == 0, 0.0, up)
             else:
                 up = fb[f, r - 1]
             if r == nrow - 1:
                 down = halo_in[1, f // 2].astype(jnp.float32)
                 down = down[(f % 2) * nlev : (f % 2 + 1) * nlev]
-                down = jnp.where(lat == bands - 1, 0.0, down)
             else:
                 down = fb[f, r + 1]
             value = x - lonp * (x - pltpu.roll(x, 1, 1))
@@ -144,8 +161,8 @@
     def flux_copy(p, off):
         target = lax.rem(lev + off, count)
         return pltpu.make_async_remote_copy(
-            src_ref=flux_out.at[p, target],
-            dst_ref=flux_in.at[p, lev],
+            src_ref=flux_out[p].at[target],
+            dst_ref=flux_in[p].at[lev],
             send_sem=flux_send_sem.at[p, off - 1],
             recv_sem=flux_recv_sem.at[p, off - 1],
             device_id={"lev": target},
@@ -165,8 +182,8 @@
     def block_copy(p, off):
         target = lax.rem(lev + off, count)
         return pltpu.make_async_remote_copy(
-            src_ref=send.at[p, target],
-            dst_ref=recv.at[p, lev],
+            src_ref=send[p].at[target],
+            dst_ref=recv[p].at[lev],
             send_sem=send_sem.at[p, off - 1],
             recv_sem=recv_sem.at[p, off - 1],
             device_id={"lev": target},
@@ -174,21 +191,26 @@
         )
 
     def finish(p):
-        for i, r in enumerate(PAIRS[p]):
+        for i, r in enumerate(STAGES[p]):
             for pair in range(nfield // 2):
                 both = jnp.concatenate([part[2 * pair, r], part[2 * pair + 1, r]], axis=0)
                 both = both.astype(jnp.bfloat16)
                 row = i * nfield * nlev + pair * 2 * nlev
                 for g in range(16):
-                    send[p, g, row : row + 2 * nlev, :] = both[:, g * 128 : (g + 1) * 128]
-        edge = flux_row[...].astype(jnp.bfloat16)
+                    send[p][g, row : row + 2 * nlev, :] = both[:, g * 128 : (g + 1) * 128]
+        edge = flux_row[0 : len(STAGES[p]) * nfield]
         for g in range(16):
-            flux_out[p, g] = edge[:, g * 128 : (g + 1) * 128]
+            flux_out[p][g] = edge[:, g * 128 : (g + 1) * 128]
         for off in ORDER:
-            flux_copy(p, off).start()
-            block_copy(p, off).start()
-        recv[p, lev] = send[p, lev]
-        flux_in[p, lev] = flux_out[p, lev]
+            late = jnp.logical_and(first_band, lax.rem(lev + off, count) == 0)
+
+            @pl.when(jnp.logical_not(late))
+            def _():
+                flux_copy(p, off).start()
+                block_copy(p, off).start()
+
+        recv[p][lev] = send[p][lev]
+        flux_in[p][lev] = flux_out[p][lev]
 
     field_copies[0].wait()
     field_copies[3].wait()
@@ -198,26 +220,28 @@
             halo_out[i, pair] = both.astype(jnp.bfloat16)
     field_copies[1].wait()
     field_copies[2].wait()
-    for k, r in enumerate(PAIRS[0]):
+    for k, r in enumerate(STAGES[0]):
         for i in range(3):
             wind_copies[i, r].wait()
         advect(r, k)
     for copy in weight_copies:
         copy.start()
 
-    pl.semaphore_wait(barrier, count + 1)
-    for i in range(2):
-        halo_copy(i).start()
+    arrivals = count - 1 - late_peer.astype(jnp.int32) + 1 - last_band.astype(jnp.int32)
+    pl.semaphore_wait(barrier, arrivals)
+
+    @pl.when(jnp.logical_not(last_band))
+    def _():
+        halo_copy(0).start()
+        pl.semaphore_signal(ready_lat, 1, device_id={"lat": south}, device_id_type=MESH)
+
+    @pl.when(late_owner)
+    def _():
+        for off in ORDER:
+            target = lax.rem(lev + off, count)
+            pl.semaphore_signal(ready_lev, 1, device_id={"lev": target}, device_id_type=MESH)
+
     finish(0)
-
-    for r in PAIRS[1]:
-        for i in range(3):
-            wind_copies[i, r].wait()
-    for i in range(2):
-        halo_copy(i).wait_recv()
-    for k, r in enumerate(PAIRS[1]):
-        advect(r, k)
-    finish(1)
 
     for copy in weight_copies:
         copy.wait()
@@ -229,23 +253,54 @@
             line = jnp.broadcast_to(src[i * 128 : (i + 1) * 128][None], (128, 128))
             dst[i * 128 : (i + 1) * 128, :] = line.T
 
+    @pl.when(jnp.logical_not(first_band))
+    def _():
+        pl.semaphore_wait(ready_lat, 1)
+        halo_copy(1).start()
+
+    for i in range(3):
+        wind_copies[i, 3].wait()
+
+    @pl.when(jnp.logical_not(last_band))
+    def _():
+        halo_copy(1).wait_recv()
+
+    advect(3, 0)
+    finish(1)
+    for i in range(3):
+        wind_copies[i, 0].wait()
+
+    @pl.when(jnp.logical_not(first_band))
+    def _():
+        halo_copy(0).wait_recv()
+
+    advect(0, 0)
+    finish(2)
+
+    @pl.when(late_peer)
+    def _():
+        pl.semaphore_wait(ready_lev, 1)
+        for p in range(len(STAGES)):
+            flux_copy(p, count - lev).start()
+            block_copy(p, count - lev).start()
+
     top = lax.broadcasted_iota(jnp.int32, (nlev, 128), 0) == 0
 
     def unpack(p):
         for off in ORDER:
             flux_copy(p, off).wait_recv()
             block_copy(p, off).wait_recv()
-        for i, r in enumerate(PAIRS[p]):
+        for i, r in enumerate(STAGES[p]):
             for pair in range(nfield // 2):
                 pieces = ([], [])
                 for g in range(16):
                     row = i * nfield * nlev + pair * 2 * nlev
-                    both = recv[p, g, row : row + 2 * nlev].astype(jnp.float32)
+                    both = recv[p][g, row : row + 2 * nlev].astype(jnp.float32)
                     for j in range(2):
                         piece = both[j * nlev : (j + 1) * nlev]
                         if g > 0:
                             k = i * nfield + 2 * pair + j
-                            edge = flux_in[p, g - 1].astype(jnp.float32)[k : k + 1]
+                            edge = flux_in[p][g - 1, k : k + 1, :]
                             edge = jnp.broadcast_to(edge, (nlev, 128))
                             piece = piece + jnp.where(top, edge, 0.0)
                         pieces[j].append(piece)
@@ -257,43 +312,52 @@
                         jnp.bfloat16
                     )
 
-    def twice(value):
-        return jnp.concatenate([value, value], axis=1)
-
     def physics(p):
-        ra, rb = PAIRS[p]
-        x = x_buf[...]
+        rows = STAGES[p]
+        cols = 128 * len(rows)
+
+        def wide(value):
+            return jnp.concatenate([value] * len(rows), axis=1)
+
+        x = x_buf[:, 0:cols]
         for start in range(0, 768, 256):
-            rows = slice(start, start + 256)
-            v = jnp.dot(w1t[rows], x, preferred_element_type=jnp.float32)
-            h1[rows] = silu(v + twice(b1[rows])).astype(jnp.bfloat16)
-        x = h1[...]
+            span = slice(start, start + 256)
+            v = jnp.dot(w1t[span], x, preferred_element_type=jnp.float32)
+            h1[span, 0:cols] = silu(v + wide(b1[span])).astype(jnp.bfloat16)
+        x = h1[:, 0:cols]
         for start in range(0, 640, 128):
-            rows = slice(start, start + 128)
-            v = jnp.dot(w2t[rows], x, preferred_element_type=jnp.float32)
-            h2[rows] = silu(v + twice(b2[rows])).astype(jnp.bfloat16)
-        x = h2[...]
+            span = slice(start, start + 128)
+            v = jnp.dot(w2t[span], x, preferred_element_type=jnp.float32)
+            h2[span, 0:cols] = silu(v + wide(b2[span])).astype(jnp.bfloat16)
+        x = h2[:, 0:cols]
         active = []
-        for r in (ra, rb):
+        for r in rows:
             hit = own_ref[0, 0, 0] == r
             for other in (own_ref[0, 0, 1], lent_ref[0, 0, 0], lent_ref[0, 0, 1]):
                 hit = jnp.logical_or(hit, other == r)
             active.append(hit)
         for start in range(0, 512, 256):
-            rows = slice(start, start + 256)
-            v = jnp.dot(w3t[rows], x, preferred_element_type=jnp.float32)
-            v = (v + twice(b3[rows])).astype(jnp.bfloat16).astype(jnp.float32)
-            for i, r in enumerate((ra, rb)):
-                out[pl.ds(start * nrow + r, 256, stride=nrow), :] = ob[r, rows] + jnp.where(
+            span = slice(start, start + 256)
+            v = jnp.dot(w3t[span], x, preferred_element_type=jnp.float32)
+            v = (v + wide(b3[span])).astype(jnp.bfloat16).astype(jnp.float32)
+            for i, r in enumerate(rows):
+                out[pl.ds(start * nrow + r, 256, stride=nrow), :] = ob[r, span] + jnp.where(
                     active[i], v[:, i * 128 : (i + 1) * 128], 0.0
                 )
 
-    for p in range(2):
+    for p in range(len(STAGES)):
         unpack(p)
         physics(p)
 
-    for p in range(2):
-        halo_copy(p).wait_send()
+    @pl.when(jnp.logical_not(last_band))
+    def _():
+        halo_copy(0).wait_send()
+
+    @pl.when(jnp.logical_not(first_band))
+    def _():
+        halo_copy(1).wait_send()
+
+    for p in range(len(STAGES)):
         for off in ORDER:
             flux_copy(p, off).wait_send()
             block_copy(p, off).wait_send()
@@ -328,6 +392,11 @@
     f32, bf16 = jnp.float32, jnp.bfloat16
     hbm = pl.BlockSpec(memory_space=pltpu.HBM)
     dma = pltpu.SemaphoreType.DMA
+    stages = len(STAGES)
+    buffers = []
+    for rows in STAGES:
+        buffers += [pltpu.VMEM((count, len(rows) * nfield, part), f32)] * 2
+        buffers += [pltpu.VMEM((count, len(rows) * nfield * nlev, part), bf16)] * 2
     return pl.pallas_call(
         kernel,
         name="tracer",
@@ -341,10 +410,7 @@
             pltpu.VMEM((2, nfield // 2, 2 * nlev, lon), bf16),
             pltpu.VMEM((2, nfield // 2, 2 * nlev, lon), bf16),
             pltpu.VMEM((2 * nfield, lon), f32),
-            pltpu.VMEM((2, count, 2 * nfield, part), bf16),
-            pltpu.VMEM((2, count, 2 * nfield, part), bf16),
-            pltpu.VMEM((2, count, 2 * nfield * nlev, part), bf16),
-            pltpu.VMEM((2, count, 2 * nfield * nlev, part), bf16),
+            *buffers,
             pltpu.VMEM((width, hidden[0]), bf16),
             pltpu.VMEM((hidden[0], hidden[1]), bf16),
             pltpu.VMEM((hidden[1], width), bf16),
@@ -368,10 +434,12 @@
             dma((8,)),
             dma((2,)),
             dma((2,)),
-            dma((2, count - 1)),
-            dma((2, count - 1)),
-            dma((2, count - 1)),
-            dma((2, count - 1)),
+            pltpu.SemaphoreType.REGULAR,
+            pltpu.SemaphoreType.REGULAR,
+            dma((stages, count - 1)),
+            dma((stages, count - 1)),
+            dma((stages, count - 1)),
+            dma((stages, count - 1)),
         ],
         compiler_params=pltpu.CompilerParams(
             collective_id=0, has_side_effects=True, vmem_limit_bytes=48 << 20

time: 38 us -> 32.7 us (0.86)
  the two profiles are of different devices: /device:TPU:1 before, /device:TPU:7 now
where the time goes in v4:
time: 32.7 us; the launch traced here: 32.6 us
  Pallas kernels  31.6 us (97%)
  local copies, waits for them, and re-layouts  0.97 us (3%)
    pallas_call x1, Pallas kernels, body(): pl.pallas_call(kernel, name='tracer', out_shape=jax.ShapeDtypeStruct((wid...  31.6 us
    unnamed x1, local copies, waits for them, and re-layouts  0.97 us

profile of v4, /device:TPU:7, one launch (start us, length us, event | category | flops | bytes accessed | tf_op | source)
XLA Modules:
  0.0 32.6 jit_solution(3812810562076104931)
XLA Ops:
  0.0 31.6 %tracer.1 = f32[2048,128]{1,0:T(8,128)S(1)} custom-call(f32[4,8,4,2048]{3,2,1,0:T(4,128)} %fields_hbm.1, f32[8,4,2048]{2,1,0:T(4,128)} %lon_hbm.1, f32[8,4,2048]{2,1,0:T(4,128)} %lat_hbm.1, f32[8,4,2048]{2,1,0:T(4,128)} %move_hbm.1, s32[1,1,2]{2,1,0:T(1,128)} %own_hbm.1, s32[1,1,2]{2,1,0:T(1,128)} %lent_hbm.1, bf16[512,768]{1,0:T(8,128)(2,1)} %w1_hbm.1, ...), custom_call_target="tpu_custom_call" | custom-call | tf_op jit(solution)/shard_map/tracer/pallas_call | solution.py:400
  31.6 1.0 %copy.14 = f32[512,4,128]{2,1,0:T(4,128)} copy(f32[512,4,128]{2,1,0:T(4,128)S(1)} %bitcast.1) | data formatting | bytes 2097152

commit v5 on v4

--- a/solution.py
+++ b/solution.py
@@ -129,34 +129,58 @@
 
     sub = lax.broadcasted_iota(jnp.int32, (nlev, lon), 0)
 
+    def halo_tile(i, f, g):
+        rows = slice((f % 2) * nlev, (f % 2 + 1) * nlev)
+        tile = halo_in[i, g % 2, f // 2, :, (g // 2) * 128 : (g // 2 + 1) * 128]
+        return tile.astype(jnp.float32)[rows]
+
+    def moved(r, cols):
+        last = jnp.logical_and(sub[:, cols] == nlev - 1, lev == count - 1)
+        return jnp.where(last, 0.0, cb[2, r, :, cols])
+
     def advect(r, k):
         lonp = jnp.maximum(cb[0, r], 0.0)
         lonn = jnp.minimum(cb[0, r], 0.0)
         latp = jnp.maximum(cb[1, r], 0.0)
         latn = jnp.minimum(cb[1, r], 0.0)
-        move = cb[2, r]
-        last = jnp.logical_and(sub == nlev - 1, lev == count - 1)
-        move = jnp.where(last, 0.0, move)
+        move = moved(r, slice(None))
         for f in range(nfield):
             x = fb[f, r]
-            if r == 0:
-                up = halo_in[0, f // 2].astype(jnp.float32)
-                up = up[(f % 2) * nlev : (f % 2 + 1) * nlev]
-            else:
-                up = fb[f, r - 1]
             if r == nrow - 1:
-                down = halo_in[1, f // 2].astype(jnp.float32)
-                down = down[(f % 2) * nlev : (f % 2 + 1) * nlev]
+                down = jnp.concatenate([halo_tile(1, f, g) for g in range(16)], axis=1)
             else:
                 down = fb[f, r + 1]
             value = x - lonp * (x - pltpu.roll(x, 1, 1))
             value = value - lonn * (pltpu.roll(x, lon - 1, 1) - x)
-            value = value - latp * (x - up)
+            if r == 0:
+                part[f, r] = value - latn * (down - x)
+                continue
+            value = value - latp * (x - fb[f, r - 1])
             value = value - latn * (down - x)
             flux = move * value
             turned = pltpu.roll(flux, 1, 0)
             part[f, r] = value - flux + jnp.where(sub == 0, 0.0, turned)
             flux_row[k * nfield + f : k * nfield + f + 1, :] = turned[0:1]
+
+    def north_row(half):
+        for g in range(half, 16, 2):
+            cols = slice(g * 128, (g + 1) * 128)
+            level = sub[:, cols]
+            latp = jnp.maximum(cb[1, 0, :, cols], 0.0)
+            move = moved(0, cols)
+            edge = jnp.zeros((nlev, 128), jnp.float32)
+            for pair in range(nfield // 2):
+                values = []
+                for f in (2 * pair, 2 * pair + 1):
+                    x = fb[f, 0, :, cols]
+                    value = part[f, 0, :, cols] - latp * (x - halo_tile(0, f, g))
+                    flux = move * value
+                    turned = pltpu.roll(flux, 1, 0)
+                    values.append(value - flux + jnp.where(level == 0, 0.0, turned))
+                    edge = jnp.where(level == f, pltpu.roll(flux, f + 1, 0), edge)
+                both = jnp.concatenate(values, axis=0).astype(jnp.bfloat16)
+                send[2][g, pair * 2 * nlev : (pair + 1) * 2 * nlev, :] = both
+            flux_out[2][g] = edge[0:nfield].astype(jnp.bfloat16)
 
     def flux_copy(p, off):
         target = lax.rem(lev + off, count)
@@ -169,12 +193,12 @@
             device_id_type=MESH,
         )
 
-    def halo_copy(i):
+    def halo_copy(i, half):
         return pltpu.make_async_remote_copy(
-            src_ref=halo_out.at[i],
-            dst_ref=halo_in.at[i],
-            send_sem=halo_send_sem.at[i],
-            recv_sem=halo_recv_sem.at[i],
+            src_ref=halo_out.at[i, half],
+            dst_ref=halo_in.at[i, half],
+            send_sem=halo_send_sem.at[i, half],
+            recv_sem=halo_recv_sem.at[i, half],
             device_id={"lat": south if i == 0 else north},
             device_id_type=MESH,
         )
@@ -198,51 +222,62 @@
                 row = i * nfield * nlev + pair * 2 * nlev
                 for g in range(16):
                     send[p][g, row : row + 2 * nlev, :] = both[:, g * 128 : (g + 1) * 128]
-        edge = flux_row[0 : len(STAGES[p]) * nfield]
+        edge = flux_row[0 : len(STAGES[p]) * nfield].astype(jnp.bfloat16)
         for g in range(16):
             flux_out[p][g] = edge[:, g * 128 : (g + 1) * 128]
+        launch(p, (0, 1))
+
+    def launch(p, halves):
         for off in ORDER:
-            late = jnp.logical_and(first_band, lax.rem(lev + off, count) == 0)
-
-            @pl.when(jnp.logical_not(late))
+            target = lax.rem(lev + off, count)
+            wanted = jnp.logical_not(jnp.logical_and(first_band, target == 0))
+            if len(halves) == 1:
+                wanted = jnp.logical_and(wanted, lax.rem(target, 2) == halves[0])
+
+            @pl.when(wanted)
             def _():
                 flux_copy(p, off).start()
                 block_copy(p, off).start()
-
-        recv[p][lev] = send[p][lev]
-        flux_in[p][lev] = flux_out[p][lev]
 
     field_copies[0].wait()
     field_copies[3].wait()
     for i, r in ((0, 3), (1, 0)):
         for pair in range(nfield // 2):
             both = jnp.concatenate([fb[2 * pair, r], fb[2 * pair + 1, r]], axis=0)
-            halo_out[i, pair] = both.astype(jnp.bfloat16)
+            both = both.astype(jnp.bfloat16)
+            for g in range(16):
+                halo_out[i, g % 2, pair, :, (g // 2) * 128 : (g // 2 + 1) * 128] = both[
+                    :, g * 128 : (g + 1) * 128
+                ]
+
+    arrivals = count - 1 - late_peer.astype(jnp.int32) + 1 - last_band.astype(jnp.int32)
+    pl.semaphore_wait(barrier, arrivals)
+
+    @pl.when(jnp.logical_not(last_band))
+    def _():
+        for half in range(2):
+            halo_copy(0, half).start()
+        pl.semaphore_signal(ready_lat, 1, device_id={"lat": south}, device_id_type=MESH)
+
+    @pl.when(late_owner)
+    def _():
+        for off in ORDER:
+            target = lax.rem(lev + off, count)
+            pl.semaphore_signal(ready_lev, 1, device_id={"lev": target}, device_id_type=MESH)
+
     field_copies[1].wait()
     field_copies[2].wait()
     for k, r in enumerate(STAGES[0]):
         for i in range(3):
             wind_copies[i, r].wait()
         advect(r, k)
+    finish(0)
+
     for copy in weight_copies:
         copy.start()
-
-    arrivals = count - 1 - late_peer.astype(jnp.int32) + 1 - last_band.astype(jnp.int32)
-    pl.semaphore_wait(barrier, arrivals)
-
-    @pl.when(jnp.logical_not(last_band))
-    def _():
-        halo_copy(0).start()
-        pl.semaphore_signal(ready_lat, 1, device_id={"lat": south}, device_id_type=MESH)
-
-    @pl.when(late_owner)
-    def _():
-        for off in ORDER:
-            target = lax.rem(lev + off, count)
-            pl.semaphore_signal(ready_lev, 1, device_id={"lev": target}, device_id_type=MESH)
-
-    finish(0)
-
+    for i in range(3):
+        wind_copies[i, 0].wait()
+    advect(0, 0)
     for copy in weight_copies:
         copy.wait()
     w1t[...] = w1[...].T
@@ -256,26 +291,27 @@
     @pl.when(jnp.logical_not(first_band))
     def _():
         pl.semaphore_wait(ready_lat, 1)
-        halo_copy(1).start()
+        for half in range(2):
+            halo_copy(1, half).start()
 
     for i in range(3):
         wind_copies[i, 3].wait()
 
     @pl.when(jnp.logical_not(last_band))
     def _():
-        halo_copy(1).wait_recv()
+        for half in range(2):
+            halo_copy(1, half).wait_recv()
 
     advect(3, 0)
     finish(1)
-    for i in range(3):
-        wind_copies[i, 0].wait()
-
-    @pl.when(jnp.logical_not(first_band))
-    def _():
-        halo_copy(0).wait_recv()
-
-    advect(0, 0)
-    finish(2)
+    for half in range(2):
+
+        @pl.when(jnp.logical_not(first_band))
+        def _():
+            halo_copy(0, half).wait_recv()
+
+        north_row(half)
+        launch(2, (half,))
 
     @pl.when(late_peer)
     def _():
@@ -287,6 +323,8 @@
     top = lax.broadcasted_iota(jnp.int32, (nlev, 128), 0) == 0
 
     def unpack(p):
+        recv[p][lev] = send[p][lev]
+        flux_in[p][lev] = flux_out[p][lev]
         for off in ORDER:
             flux_copy(p, off).wait_recv()
             block_copy(p, off).wait_recv()
@@ -300,7 +338,7 @@
                         piece = both[j * nlev : (j + 1) * nlev]
                         if g > 0:
                             k = i * nfield + 2 * pair + j
-                            edge = flux_in[p][g - 1, k : k + 1, :]
+                            edge = flux_in[p][g - 1].astype(jnp.float32)[k : k + 1]
                             edge = jnp.broadcast_to(edge, (nlev, 128))
                             piece = piece + jnp.where(top, edge, 0.0)
                         pieces[j].append(piece)
@@ -351,11 +389,13 @@
 
     @pl.when(jnp.logical_not(last_band))
     def _():
-        halo_copy(0).wait_send()
+        for half in range(2):
+            halo_copy(0, half).wait_send()
 
     @pl.when(jnp.logical_not(first_band))
     def _():
-        halo_copy(1).wait_send()
+        for half in range(2):
+            halo_copy(1, half).wait_send()
 
     for p in range(len(STAGES)):
         for off in ORDER:
@@ -395,7 +435,7 @@
     stages = len(STAGES)
     buffers = []
     for rows in STAGES:
-        buffers += [pltpu.VMEM((count, len(rows) * nfield, part), f32)] * 2
+        buffers += [pltpu.VMEM((count, len(rows) * nfield, part), bf16)] * 2
         buffers += [pltpu.VMEM((count, len(rows) * nfield * nlev, part), bf16)] * 2
     return pl.pallas_call(
         kernel,
@@ -407,8 +447,8 @@
             pltpu.VMEM((nfield, nrow, nlev, lon), f32),
             pltpu.VMEM((3, nrow, nlev, lon), f32),
             pltpu.VMEM((nfield, nrow, nlev, lon), f32),
-            pltpu.VMEM((2, nfield // 2, 2 * nlev, lon), bf16),
-            pltpu.VMEM((2, nfield // 2, 2 * nlev, lon), bf16),
+            pltpu.VMEM((2, 2, nfield // 2, 2 * nlev, lon // 2), bf16),
+            pltpu.VMEM((2, 2, nfield // 2, 2 * nlev, lon // 2), bf16),
             pltpu.VMEM((2 * nfield, lon), f32),
             *buffers,
             pltpu.VMEM((width, hidden[0]), bf16),
@@ -432,8 +472,8 @@
             dma((nrow,)),
             dma((3, nrow)),
             dma((8,)),
-            dma((2,)),
-            dma((2,)),
+            dma((2, 2)),
+            dma((2, 2)),
             pltpu.SemaphoreType.REGULAR,
             pltpu.SemaphoreType.REGULAR,
             dma((stages, count - 1)),

time: 32.7 us -> 31.9 us (0.976)
  Pallas kernels: 31.6 us -> 30.7 us
    pallas_call x1, Pallas kernels: 31.6 us -> 30.7 us  [body(): pl.pallas_call(kernel, name='tracer', out_shape=jax.ShapeDtypeStruct((wid...]
where the time goes in v5:
time: 31.9 us; the launch traced here: 31.7 us
  Pallas kernels  30.7 us (96%)
  local copies, waits for them, and re-layouts  0.97 us (3%)
    pallas_call x1, Pallas kernels, body(): pl.pallas_call(kernel, name='tracer', out_shape=jax.ShapeDtypeStruct((wid...  30.7 us
    unnamed x1, local copies, waits for them, and re-layouts  0.97 us

profile of v5, /device:TPU:7, one launch (start us, length us, event | category | flops | bytes accessed | tf_op | source)
XLA Modules:
  0.0 31.7 jit_solution(17626712319080928805)
XLA Ops:
  0.0 30.7 %tracer.1 = f32[2048,128]{1,0:T(8,128)S(1)} custom-call(f32[4,8,4,2048]{3,2,1,0:T(4,128)} %fields_hbm.1, f32[8,4,2048]{2,1,0:T(4,128)} %lon_hbm.1, f32[8,4,2048]{2,1,0:T(4,128)} %lat_hbm.1, f32[8,4,2048]{2,1,0:T(4,128)} %move_hbm.1, s32[1,1,2]{2,1,0:T(1,128)} %own_hbm.1, s32[1,1,2]{2,1,0:T(1,128)} %lent_hbm.1, bf16[512,768]{1,0:T(8,128)(2,1)} %w1_hbm.1, ...), custom_call_target="tpu_custom_call" | custom-call | tf_op jit(solution)/shard_map/tracer/pallas_call | solution.py:440
  30.7 1.0 %copy.14 = f32[512,4,128]{2,1,0:T(4,128)} copy(f32[512,4,128]{2,1,0:T(4,128)S(1)} %bitcast.1) | data formatting | bytes 2097152

commit v6 on v5

--- a/solution.py
+++ b/solution.py
@@ -61,7 +61,8 @@
         weight_sem,
         halo_send_sem,
         halo_recv_sem,
-        ready_lat,
+        ready_north,
+        ready_south,
         ready_lev,
         flux_send_sem,
         flux_recv_sem,
@@ -115,7 +116,22 @@
             target = lax.rem(lev + off, count)
             pl.semaphore_signal(barrier, 1, device_id={"lev": target}, device_id_type=MESH)
 
-    @pl.when(jnp.logical_not(first_band))
+    run = bands // 4
+    place = lax.rem(lat, run)
+    odd_south = jnp.logical_or(place == run - 1, late_owner)
+    odd_north = jnp.logical_or(place == 0, jnp.logical_and(lat == 1, lev == 0))
+    has_south = jnp.logical_not(last_band)
+    has_north = jnp.logical_not(first_band)
+    south_first = jnp.logical_and(has_south, odd_south)
+    south_later = jnp.logical_and(has_south, jnp.logical_not(odd_south))
+    north_first = jnp.logical_and(has_north, jnp.logical_not(odd_north))
+    north_later = jnp.logical_and(has_north, odd_north)
+
+    @pl.when(south_later)
+    def _():
+        pl.semaphore_signal(barrier, 1, device_id={"lat": south}, device_id_type=MESH)
+
+    @pl.when(north_later)
     def _():
         pl.semaphore_signal(barrier, 1, device_id={"lat": north}, device_id_type=MESH)
 
@@ -230,9 +246,10 @@
     def launch(p, halves):
         for off in ORDER:
             target = lax.rem(lev + off, count)
-            wanted = jnp.logical_not(jnp.logical_and(first_band, target == 0))
             if len(halves) == 1:
-                wanted = jnp.logical_and(wanted, lax.rem(target, 2) == halves[0])
+                wanted = lax.rem(target, 2) == halves[0]
+            else:
+                wanted = jnp.logical_not(jnp.logical_and(first_band, target == 0))
 
             @pl.when(wanted)
             def _():
@@ -250,14 +267,28 @@
                     :, g * 128 : (g + 1) * 128
                 ]
 
-    arrivals = count - 1 - late_peer.astype(jnp.int32) + 1 - last_band.astype(jnp.int32)
+    for copy in weight_copies:
+        copy.start()
+
+    def send_row(i, ready=None):
+        if ready is not None:
+            pl.semaphore_wait(ready, 1)
+        for half in range(2):
+            halo_copy(i, half).start()
+
+    arrivals = count - 1 - late_peer.astype(jnp.int32)
+    arrivals = arrivals + south_first.astype(jnp.int32) + north_first.astype(jnp.int32)
     pl.semaphore_wait(barrier, arrivals)
 
-    @pl.when(jnp.logical_not(last_band))
-    def _():
-        for half in range(2):
-            halo_copy(0, half).start()
-        pl.semaphore_signal(ready_lat, 1, device_id={"lat": south}, device_id_type=MESH)
+    @pl.when(south_first)
+    def _():
+        send_row(0)
+        pl.semaphore_signal(ready_north, 1, device_id={"lat": south}, device_id_type=MESH)
+
+    @pl.when(north_first)
+    def _():
+        send_row(1)
+        pl.semaphore_signal(ready_south, 1, device_id={"lat": north}, device_id_type=MESH)
 
     @pl.when(late_owner)
     def _():
@@ -273,8 +304,6 @@
         advect(r, k)
     finish(0)
 
-    for copy in weight_copies:
-        copy.start()
     for i in range(3):
         wind_copies[i, 0].wait()
     advect(0, 0)
@@ -288,11 +317,9 @@
             line = jnp.broadcast_to(src[i * 128 : (i + 1) * 128][None], (128, 128))
             dst[i * 128 : (i + 1) * 128, :] = line.T
 
-    @pl.when(jnp.logical_not(first_band))
-    def _():
-        pl.semaphore_wait(ready_lat, 1)
-        for half in range(2):
-            halo_copy(1, half).start()
+    @pl.when(south_later)
+    def _():
+        send_row(0, ready_south)
 
     for i in range(3):
         wind_copies[i, 3].wait()
@@ -304,6 +331,18 @@
 
     advect(3, 0)
     finish(1)
+
+    @pl.when(late_peer)
+    def _():
+        pl.semaphore_wait(ready_lev, 1)
+        for p in range(2):
+            flux_copy(p, count - lev).start()
+            block_copy(p, count - lev).start()
+
+    @pl.when(north_later)
+    def _():
+        send_row(1, ready_north)
+
     for half in range(2):
 
         @pl.when(jnp.logical_not(first_band))
@@ -312,13 +351,6 @@
 
         north_row(half)
         launch(2, (half,))
-
-    @pl.when(late_peer)
-    def _():
-        pl.semaphore_wait(ready_lev, 1)
-        for p in range(len(STAGES)):
-            flux_copy(p, count - lev).start()
-            block_copy(p, count - lev).start()
 
     top = lax.broadcasted_iota(jnp.int32, (nlev, 128), 0) == 0
 
@@ -476,6 +508,7 @@
             dma((2, 2)),
             pltpu.SemaphoreType.REGULAR,
             pltpu.SemaphoreType.REGULAR,
+            pltpu.SemaphoreType.REGULAR,
             dma((stages, count - 1)),
             dma((stages, count - 1)),
             dma((stages, count - 1)),

time: 31.9 us -> 31.2 us (0.978)
  Pallas kernels: 30.7 us -> 30 us
    pallas_call x1, Pallas kernels: 30.7 us -> 30 us  [body(): pl.pallas_call(kernel, name='tracer', out_shape=jax.ShapeDtypeStruct((wid...]
where the time goes in v6:
time: 31.2 us; the launch traced here: 31 us
  Pallas kernels  30 us (96%)
  local copies, waits for them, and re-layouts  0.97 us (3%)
    pallas_call x1, Pallas kernels, body(): pl.pallas_call(kernel, name='tracer', out_shape=jax.ShapeDtypeStruct((wid...  30 us
    unnamed x1, local copies, waits for them, and re-layouts  0.97 us

profile of v6, /device:TPU:7, one launch (start us, length us, event | category | flops | bytes accessed | tf_op | source)
XLA Modules:
  0.0 31.0 jit_solution(397485906214701464)
XLA Ops:
  0.0 30.0 %tracer.1 = f32[2048,128]{1,0:T(8,128)S(1)} custom-call(f32[4,8,4,2048]{3,2,1,0:T(4,128)} %fields_hbm.1, f32[8,4,2048]{2,1,0:T(4,128)} %lon_hbm.1, f32[8,4,2048]{2,1,0:T(4,128)} %lat_hbm.1, f32[8,4,2048]{2,1,0:T(4,128)} %move_hbm.1, s32[1,1,2]{2,1,0:T(1,128)} %own_hbm.1, s32[1,1,2]{2,1,0:T(1,128)} %lent_hbm.1, bf16[512,768]{1,0:T(8,128)(2,1)} %w1_hbm.1, ...), custom_call_target="tpu_custom_call" | custom-call | tf_op jit(solution)/shard_map/tracer/pallas_call | solution.py:472
  30.0 1.0 %copy.14 = f32[512,4,128]{2,1,0:T(4,128)} copy(f32[512,4,128]{2,1,0:T(4,128)S(1)} %bitcast.1) | data formatting | bytes 2097152

commit v7 on v6

--- a/solution.py
+++ b/solution.py
@@ -76,6 +76,38 @@
     north, south = lax.rem(lat + bands - 1, bands), lax.rem(lat + 1, bands)
     nfield, nrow, nlev, lon = fb.shape
 
+    first_band = lat == 0
+    last_band = lat == bands - 1
+    late_owner = jnp.logical_and(first_band, lev == 0)
+    late_peer = jnp.logical_and(first_band, lev != 0)
+
+    barrier = pltpu.get_barrier_semaphore()
+
+    @pl.when(jnp.logical_not(late_owner))
+    def _():
+        for off in ORDER:
+            target = lax.rem(lev + off, count)
+            pl.semaphore_signal(barrier, 1, device_id={"lev": target}, device_id_type=MESH)
+
+    run = bands // 4
+    place = lax.rem(lat, run)
+    odd_south = jnp.logical_or(place == run - 1, late_owner)
+    odd_north = jnp.logical_or(place == 0, jnp.logical_and(lat == 1, lev == 0))
+    has_south = jnp.logical_not(last_band)
+    has_north = jnp.logical_not(first_band)
+    south_first = jnp.logical_and(has_south, odd_south)
+    south_later = jnp.logical_and(has_south, jnp.logical_not(odd_south))
+    north_first = jnp.logical_and(has_north, jnp.logical_not(odd_north))
+    north_later = jnp.logical_and(has_north, odd_north)
+
+    @pl.when(south_later)
+    def _():
+        pl.semaphore_signal(barrier, 1, device_id={"lat": south}, device_id_type=MESH)
+
+    @pl.when(north_later)
+    def _():
+        pl.semaphore_signal(barrier, 1, device_id={"lat": north}, device_id_type=MESH)
+
     field_copies = {}
     wind_copies = {}
     for r in (0, 3, 1, 2):
@@ -86,7 +118,7 @@
     for r in (1, 2, 0, 3):
         for i, src in enumerate((lon_hbm, lat_hbm, move_hbm)):
             wind_copies[i, r] = pltpu.make_async_copy(
-                src.at[:, r, :], cb.at[i, r], wind_sem.at[i, r]
+                src.at[:, r, :], cb.at[i, r], wind_sem.at[r]
             )
             wind_copies[i, r].start()
     weight_copies = []
@@ -102,38 +134,6 @@
     )
     for i, (src, dst) in enumerate(moves):
         weight_copies.append(pltpu.make_async_copy(src, dst, weight_sem.at[i]))
-
-    first_band = lat == 0
-    last_band = lat == bands - 1
-    late_owner = jnp.logical_and(first_band, lev == 0)
-    late_peer = jnp.logical_and(first_band, lev != 0)
-
-    barrier = pltpu.get_barrier_semaphore()
-
-    @pl.when(jnp.logical_not(late_owner))
-    def _():
-        for off in ORDER:
-            target = lax.rem(lev + off, count)
-            pl.semaphore_signal(barrier, 1, device_id={"lev": target}, device_id_type=MESH)
-
-    run = bands // 4
-    place = lax.rem(lat, run)
-    odd_south = jnp.logical_or(place == run - 1, late_owner)
-    odd_north = jnp.logical_or(place == 0, jnp.logical_and(lat == 1, lev == 0))
-    has_south = jnp.logical_not(last_band)
-    has_north = jnp.logical_not(first_band)
-    south_first = jnp.logical_and(has_south, odd_south)
-    south_later = jnp.logical_and(has_south, jnp.logical_not(odd_south))
-    north_first = jnp.logical_and(has_north, jnp.logical_not(odd_north))
-    north_later = jnp.logical_and(has_north, odd_north)
-
-    @pl.when(south_later)
-    def _():
-        pl.semaphore_signal(barrier, 1, device_id={"lat": south}, device_id_type=MESH)
-
-    @pl.when(north_later)
-    def _():
-        pl.semaphore_signal(barrier, 1, device_id={"lat": north}, device_id_type=MESH)
 
     @pl.when(first_band)
     def _():
@@ -203,8 +203,8 @@
         return pltpu.make_async_remote_copy(
             src_ref=flux_out[p].at[target],
             dst_ref=flux_in[p].at[lev],
-            send_sem=flux_send_sem.at[p, off - 1],
-            recv_sem=flux_recv_sem.at[p, off - 1],
+            send_sem=flux_send_sem.at[p],
+            recv_sem=flux_recv_sem.at[p],
             device_id={"lev": target},
             device_id_type=MESH,
         )
@@ -224,11 +224,19 @@
         return pltpu.make_async_remote_copy(
             src_ref=send[p].at[target],
             dst_ref=recv[p].at[lev],
-            send_sem=send_sem.at[p, off - 1],
-            recv_sem=recv_sem.at[p, off - 1],
+            send_sem=send_sem.at[p],
+            recv_sem=recv_sem.at[p],
             device_id={"lev": target},
             device_id_type=MESH,
         )
+
+    def await_winds(r):
+        row = cb.at[:, r]
+        pltpu.make_async_copy(row, row, wind_sem.at[r]).wait()
+
+    def await_all(ref, sem):
+        rows = ref.at[pl.ds(0, count - 1)]
+        pltpu.make_async_copy(rows, rows, sem).wait()
 
     def finish(p):
         for i, r in enumerate(STAGES[p]):
@@ -299,13 +307,11 @@
     field_copies[1].wait()
     field_copies[2].wait()
     for k, r in enumerate(STAGES[0]):
-        for i in range(3):
-            wind_copies[i, r].wait()
+        await_winds(r)
         advect(r, k)
     finish(0)
 
-    for i in range(3):
-        wind_copies[i, 0].wait()
+    await_winds(0)
     advect(0, 0)
     for copy in weight_copies:
         copy.wait()
@@ -321,8 +327,7 @@
     def _():
         send_row(0, ready_south)
 
-    for i in range(3):
-        wind_copies[i, 3].wait()
+    await_winds(3)
 
     @pl.when(jnp.logical_not(last_band))
     def _():
@@ -352,14 +357,28 @@
         north_row(half)
         launch(2, (half,))
 
+    def drain():
+        @pl.when(has_south)
+        def _():
+            for half in range(2):
+                halo_copy(0, half).wait_send()
+
+        @pl.when(has_north)
+        def _():
+            for half in range(2):
+                halo_copy(1, half).wait_send()
+
+        for p in range(len(STAGES)):
+            await_all(flux_out[p], flux_send_sem.at[p])
+            await_all(send[p], send_sem.at[p])
+
     top = lax.broadcasted_iota(jnp.int32, (nlev, 128), 0) == 0
 
     def unpack(p):
+        await_all(flux_in[p], flux_recv_sem.at[p])
+        await_all(recv[p], recv_sem.at[p])
         recv[p][lev] = send[p][lev]
         flux_in[p][lev] = flux_out[p][lev]
-        for off in ORDER:
-            flux_copy(p, off).wait_recv()
-            block_copy(p, off).wait_recv()
         for i, r in enumerate(STAGES[p]):
             for pair in range(nfield // 2):
                 pieces = ([], [])
@@ -416,23 +435,10 @@
                 )
 
     for p in range(len(STAGES)):
+        if p == len(STAGES) - 1:
+            drain()
         unpack(p)
         physics(p)
-
-    @pl.when(jnp.logical_not(last_band))
-    def _():
-        for half in range(2):
-            halo_copy(0, half).wait_send()
-
-    @pl.when(jnp.logical_not(first_band))
-    def _():
-        for half in range(2):
-            halo_copy(1, half).wait_send()
-
-    for p in range(len(STAGES)):
-        for off in ORDER:
-            flux_copy(p, off).wait_send()
-            block_copy(p, off).wait_send()
 
 
 ORDER = (8, 7, 9, 6, 10, 5, 11, 4, 12, 3, 13, 2, 14, 1, 15)
@@ -502,17 +508,17 @@
             pltpu.VMEM(bias_second.shape, f32),
             pltpu.VMEM(bias_third.shape, f32),
             dma((nrow,)),
-            dma((3, nrow)),
+            dma((nrow,)),
             dma((8,)),
             dma((2, 2)),
             dma((2, 2)),
             pltpu.SemaphoreType.REGULAR,
             pltpu.SemaphoreType.REGULAR,
             pltpu.SemaphoreType.REGULAR,
-            dma((stages, count - 1)),
-            dma((stages, count - 1)),
-            dma((stages, count - 1)),
-            dma((stages, count - 1)),
+            dma((stages,)),
+            dma((stages,)),
+            dma((stages,)),
+            dma((stages,)),
         ],
         compiler_params=pltpu.CompilerParams(
             collective_id=0, has_side_effects=True, vmem_limit_bytes=48 << 20

time: 31.2 us -> 29.4 us (0.942)
  Pallas kernels: 30 us -> 28.2 us
    pallas_call x1, Pallas kernels: 30 us -> 28.2 us  [body(): pl.pallas_call(kernel, name='tracer', out_shape=jax.ShapeDtypeStruct((wid...]
where the time goes in v7:
time: 29.4 us; the launch traced here: 29.2 us
  Pallas kernels  28.2 us (96%)
  local copies, waits for them, and re-layouts  0.97 us (3%)
    pallas_call x1, Pallas kernels, body(): pl.pallas_call(kernel, name='tracer', out_shape=jax.ShapeDtypeStruct((wid...  28.2 us
    unnamed x1, local copies, waits for them, and re-layouts  0.97 us

profile of v7, /device:TPU:7, one launch (start us, length us, event | category | flops | bytes accessed | tf_op | source)
XLA Modules:
  0.0 29.2 jit_solution(14605872139358051830)
XLA Ops:
  0.0 28.2 %tracer.1 = f32[2048,128]{1,0:T(8,128)S(1)} custom-call(f32[4,8,4,2048]{3,2,1,0:T(4,128)} %fields_hbm.1, f32[8,4,2048]{2,1,0:T(4,128)} %lon_hbm.1, f32[8,4,2048]{2,1,0:T(4,128)} %lat_hbm.1, f32[8,4,2048]{2,1,0:T(4,128)} %move_hbm.1, s32[1,1,2]{2,1,0:T(1,128)} %own_hbm.1, s32[1,1,2]{2,1,0:T(1,128)} %lent_hbm.1, bf16[512,768]{1,0:T(8,128)(2,1)} %w1_hbm.1, ...), custom_call_target="tpu_custom_call" | custom-call | tf_op jit(solution)/shard_map/tracer/pallas_call | solution.py:478
  28.2 1.0 %copy.14 = f32[512,4,128]{2,1,0:T(4,128)} copy(f32[512,4,128]{2,1,0:T(4,128)S(1)} %bitcast.1) | data formatting | bytes 2097152

commit v8 on v7

--- a/solution.py
+++ b/solution.py
@@ -61,6 +61,8 @@
         weight_sem,
         halo_send_sem,
         halo_recv_sem,
+        ring_count,
+        ring_ready,
         ready_north,
         ready_south,
         ready_lev,
@@ -83,18 +85,21 @@
 
     barrier = pltpu.get_barrier_semaphore()
 
-    @pl.when(jnp.logical_not(late_owner))
+    run = bands // 4
+    place = lax.rem(lat, run)
+    has_south = jnp.logical_not(last_band)
+    has_north = jnp.logical_not(first_band)
+    told = jnp.logical_and(place == run - 1, has_south)
+    teller = jnp.logical_and(place == 0, has_north)
+
+    @pl.when(jnp.logical_not(jnp.logical_or(late_owner, told)))
     def _():
         for off in ORDER:
             target = lax.rem(lev + off, count)
             pl.semaphore_signal(barrier, 1, device_id={"lev": target}, device_id_type=MESH)
 
-    run = bands // 4
-    place = lax.rem(lat, run)
     odd_south = jnp.logical_or(place == run - 1, late_owner)
     odd_north = jnp.logical_or(place == 0, jnp.logical_and(lat == 1, lev == 0))
-    has_south = jnp.logical_not(last_band)
-    has_north = jnp.logical_not(first_band)
     south_first = jnp.logical_and(has_south, odd_south)
     south_later = jnp.logical_and(has_south, jnp.logical_not(odd_south))
     north_first = jnp.logical_and(has_north, jnp.logical_not(odd_north))
@@ -249,6 +254,12 @@
         edge = flux_row[0 : len(STAGES[p]) * nfield].astype(jnp.bfloat16)
         for g in range(16):
             flux_out[p][g] = edge[:, g * 128 : (g + 1) * 128]
+        if p == 0:
+
+            @pl.when(told)
+            def _():
+                pl.semaphore_wait(ring_ready, 1)
+
         launch(p, (0, 1))
 
     def launch(p, halves):
@@ -284,7 +295,7 @@
         for half in range(2):
             halo_copy(i, half).start()
 
-    arrivals = count - 1 - late_peer.astype(jnp.int32)
+    arrivals = (count - 1) * (1 - told.astype(jnp.int32)) - late_peer.astype(jnp.int32)
     arrivals = arrivals + south_first.astype(jnp.int32) + north_first.astype(jnp.int32)
     pl.semaphore_wait(barrier, arrivals)
 
@@ -347,6 +358,14 @@
     @pl.when(north_later)
     def _():
         send_row(1, ready_north)
+
+    @pl.when(teller)
+    def _():
+        for off in ORDER:
+            target = lax.rem(lev + off, count)
+            pl.semaphore_signal(ring_count, 1, device_id={"lev": target}, device_id_type=MESH)
+        pl.semaphore_wait(ring_count, count - 1)
+        pl.semaphore_signal(ring_ready, 1, device_id={"lat": north}, device_id_type=MESH)
 
     for half in range(2):
 
@@ -512,9 +531,7 @@
             dma((8,)),
             dma((2, 2)),
             dma((2, 2)),
-            pltpu.SemaphoreType.REGULAR,
-            pltpu.SemaphoreType.REGULAR,
-            pltpu.SemaphoreType.REGULAR,
+            *[pltpu.SemaphoreType.REGULAR] * 5,
             dma((stages,)),
             dma((stages,)),
             dma((stages,)),

time: 29.4 us -> 29.3 us (level)
  no operation moved by 1% of the time
where the time goes in v8:
time: 29.3 us; the launch traced here: 29.1 us
  Pallas kernels  28.2 us (96%)
  local copies, waits for them, and re-layouts  0.97 us (3%)
    pallas_call x1, Pallas kernels, body(): pl.pallas_call(kernel, name='tracer', out_shape=jax.ShapeDtypeStruct((wid...  28.2 us
    unnamed x1, local copies, waits for them, and re-layouts  0.97 us

profile of v8, /device:TPU:7, one launch (start us, length us, event | category | flops | bytes accessed | tf_op | source)
XLA Modules:
  0.0 29.1 jit_solution(1941598531292496695)
XLA Ops:
  0.0 28.2 %tracer.1 = f32[2048,128]{1,0:T(8,128)S(1)} custom-call(f32[4,8,4,2048]{3,2,1,0:T(4,128)} %fields_hbm.1, f32[8,4,2048]{2,1,0:T(4,128)} %lon_hbm.1, f32[8,4,2048]{2,1,0:T(4,128)} %lat_hbm.1, f32[8,4,2048]{2,1,0:T(4,128)} %move_hbm.1, s32[1,1,2]{2,1,0:T(1,128)} %own_hbm.1, s32[1,1,2]{2,1,0:T(1,128)} %lent_hbm.1, bf16[512,768]{1,0:T(8,128)(2,1)} %w1_hbm.1, ...), custom_call_target="tpu_custom_call" | custom-call | tf_op jit(solution)/shard_map/tracer/pallas_call | solution.py:497
  28.2 1.0 %copy.14 = f32[512,4,128]{2,1,0:T(4,128)} copy(f32[512,4,128]{2,1,0:T(4,128)S(1)} %bitcast.1) | data formatting | bytes 2097152
